TPU v7x, 128 devices: a whole 4x4x4 slice. The times are simulated.
128 devices in a mesh: seq: 16 (over x_lo, z, core), tp: 8 (over y, x_hi).
Axes of the slice: x: 4 (x_hi: 2, x_lo: 2; x = x_hi * 2 + x_lo), y: 4, z: 4, core: 2. Of those that a mesh axis runs over, the one named last changes fastest.
Arguments:
- hidden_in: bfloat16 [6144, 3584], P('seq'), may hold values from -48 to 48
- joined_inputs: bfloat16 [6144, 8192], P('seq', 'tp'), may hold values from -64 to 64
- lengths: int32 [4], replicated, may hold values from 1 to 3072, 6144 in all
- o_weight: bfloat16 [4096, 3584], P('tp'), may hold values from -0.09375 to 0.09375
- gate_up: float32 [2, 3584, 7168], P(None, ('seq', 'tp')), may hold values from -0.09375 to 0.09375
- down_weight: bfloat16 [7168, 3584], P('tp'), may hold values from -0.0625 to 0.0625
- next_weight: bfloat16 [3584, 8192], P(None, 'tp'), may hold values from -0.09375 to 0.09375
- post_attn_gain: float32 [3584], replicated, may hold values from 0.1 to 1.9
- pre_ffw_gain: float32 [3584], replicated, may hold values from 0.1 to 1.9
- post_ffw_gain: float32 [3584], replicated, may hold values from 0.1 to 1.9
- next_gain: float32 [3584], replicated, may hold values from 0.1 to 1.9
Outputs:
- next_qkv: bfloat16 [6144, 8192], P('seq', 'tp')
Inputs may be any that keep to these rules, and one draw needn't show every extreme that they name: The lengths of 4 prompts laid end to end; they sum to 6144 and the longest is exactly 3072.
All inputs are finite; a program needn't handle non-finite values.
Results may differ from a plain program's by a relative error of at most 0.022.
Values may be sent and summed in bfloat16 or wider, within the bound.
A program may use at most 192 MiB of HBM per device.

v0:
```python
import jax
import jax.numpy as jnp
from jax import lax
from jax.sharding import PartitionSpec as P

HEADS = 16
KV_HEADS = 8
HEAD_DIM = 256


def rms_norm(values, gain):
    meansq = jnp.mean(values * values, axis=-1, keepdims=True)
    return values * lax.rsqrt(meansq + 1e-06) * gain


def local(
    hidden_in,
    joined_inputs,
    lengths,
    o_weight,
    gate_up,
    down_weight,
    next_weight,
    post_attn_gain,
    pre_ffw_gain,
    post_ffw_gain,
    next_gain,
):
    seq_count = lax.axis_size("seq")
    tp_count = lax.axis_size("tp")
    row_count = hidden_in.shape[0]
    model_width = hidden_in.shape[1]
    per_group = HEADS // KV_HEADS
    group_cols = (per_group + 2) * HEAD_DIM
    local_groups = joined_inputs.shape[1] // group_cols
    grouped = joined_inputs.reshape(row_count, local_groups, group_cols)
    queries = grouped[:, :, : per_group * HEAD_DIM].reshape(
        row_count, local_groups, per_group, HEAD_DIM
    )
    own_keys = grouped[:, :, per_group * HEAD_DIM : (per_group + 1) * HEAD_DIM]
    own_values = grouped[:, :, (per_group + 1) * HEAD_DIM :]
    keys_all, values_all = (
        lax.all_gather(own_keys, "seq", axis=0, tiled=True),
        lax.all_gather(own_values, "seq", axis=0, tiled=True),
    )
    total_rows = keys_all.shape[0]
    seq_index = lax.axis_index("seq")
    position = seq_index * row_count
    ends = jnp.cumsum(lengths)
    places = jnp.arange(total_rows, dtype=jnp.int32)
    prompt_ids = jnp.sum((places[:, None] >= ends[None, :]).astype(jnp.int32), axis=1)
    query_place = position + jnp.arange(row_count, dtype=jnp.int32)
    query_ids = lax.dynamic_slice_in_dim(prompt_ids, position, row_count, 0)
    scale = HEAD_DIM ** (-0.5)
    scores = (
        jnp.einsum("qgrd,kgd->qgrk", queries, keys_all, preferred_element_type=jnp.float32) * scale
    )
    allowed = (
        (query_ids[:, None] == prompt_ids[None, :]) & (places[None, :] <= query_place[:, None])
    )[:, None, None, :]
    scores = jnp.where(allowed, scores, -jnp.inf)
    peak = jnp.max(scores, axis=-1, keepdims=True)
    weights = jnp.where(allowed, jnp.exp(scores - peak), 0.0)
    norm_sum = jnp.sum(weights, axis=-1)
    blended = jnp.einsum(
        "qgrk,kgd->qgrd",
        weights.astype(jnp.bfloat16),
        values_all,
        preferred_element_type=jnp.float32,
    )
    blended = blended / norm_sum[..., None]
    attended = blended.astype(jnp.bfloat16).reshape(row_count, local_groups * per_group * HEAD_DIM)
    projected = jnp.dot(attended, o_weight, preferred_element_type=jnp.float32)

    def total_of(values):
        return lax.psum(values.astype(jnp.bfloat16), "tp").astype(jnp.float32)

    residual_mid = hidden_in.astype(jnp.float32) + rms_norm(total_of(projected), post_attn_gain)
    ffw_in = rms_norm(residual_mid, pre_ffw_gain).astype(jnp.bfloat16)
    server_low = gate_up.astype(jnp.bfloat16)
    stacked_rows = lax.all_gather(server_low, "seq", axis=1, tiled=True)
    local_units = lax.all_to_all(stacked_rows, "tp", split_axis=2, concat_axis=1, tiled=True)
    piece_rows = gate_up.shape[1]
    reordered = (
        ffw_in.reshape(row_count, seq_count, tp_count, piece_rows)
        .transpose(0, 2, 1, 3)
        .reshape(row_count, model_width)
    )
    gate = jnp.dot(reordered, local_units[0], preferred_element_type=jnp.float32)
    up_part = jnp.dot(reordered, local_units[1], preferred_element_type=jnp.float32)
    activated = (jax.nn.gelu(gate, approximate=True) * up_part).astype(jnp.bfloat16)
    ffw_out = jnp.dot(activated, down_weight, preferred_element_type=jnp.float32)
    residual_out = residual_mid + rms_norm(total_of(ffw_out), post_ffw_gain)
    next_in = rms_norm(residual_out, next_gain).astype(jnp.bfloat16)
    return jnp.dot(next_in, next_weight, preferred_element_type=jnp.float32).astype(jnp.bfloat16)


def solution(mesh):
    in_specs = (
        P("seq", None),
        P("seq", "tp"),
        P(),
        P("tp", None),
        P(None, ("seq", "tp"), None),
        P("tp", None),
        P(None, "tp"),
        P(),
        P(),
        P(),
        P(),
    )
    out_specs = P("seq", "tp")
    return jax.shard_map(local, mesh=mesh, in_specs=in_specs, out_specs=out_specs, check_vma=False)
```

profile of v0, /device:TPU:1, one launch (start us, length us, event | category | flops | bytes accessed | tf_op | source)
XLA Modules:
  0.0 658.8 jit_solution(18442453555862474000)
XLA Ops:
  14.4 72.0 %all-gather.8.cloned.1.call-done = bf16[2,448,7168]{2,0,1:T(2,128)(2,1)} async-done(((bf16[2,28,7168]{2,0,1:T(2,128)(2,1)}), bf16[2,448,7168]{2,0,1:T(2,128)(2,1)}) %all-gather.8.cloned.1.call-update) | async-done | bytes 12845072 | tf_op jit(solution)/shard_map/all_gather | solution.py:81
  86.4 48.5 %copy.55 = bf16[2,448,7168]{1,0,2:T(2,128)(2,1)} copy(bf16[2,448,7168]{2,0,1:T(2,128)(2,1)} %all-gather.8.cloned.1.call-done) | data formatting | bytes 25690112 | tf_op jit(solution)/shard_map/all_gather | solution.py:81
  134.9 6.5 all-to-all-start
  141.5 3.8 fusion.6
  145.2 5.4 fusion
  150.7 6.5 copy-done.2
  157.2 6.1 fusion.1
  163.3 4.7 all-gather.6.cloned.1.call-done
  167.9 13.2 %fusion.39 = bf16[1,256,384,2]{2,1,3,0:T(8,128)(2,1)S(1)} fusion(bf16[6144,1,256]{2,0,1:T(8,128)(2,1)} %all-gather.6.cloned.1.call-done, f32[6144,384,2]{1,0,2:T(8,128)} %copy-done.2, f32[384,2]{0,1:T(2,128)S(1)} %get-tuple-element.9, pred[384,6144]{0,1:T(8,128)(4,1)} %fusion.6, f32[384,2]{0,1:T(2,128)S(1)} %fusion.1), kind=kOutput, calls=%fused_computation.45 | convolution fusion | flops 2439905280 | bytes 24778752 | tf_op jit(solution)/shard_map/qgrk,kgd->qgrd/dot_general | solution.py:65
  184.6 232.3 %all-reduce.3.cloned.1.call-done = bf16[384,3584]{1,0:T(8,128)(2,1)} async-done(((bf16[384,3584]{1,0:T(8,128)(2,1)}), bf16[384,3584]{1,0:T(8,128)(2,1)}) %all-reduce.3.cloned.1.call-update) | async-done | bytes 2752528 | tf_op jit(solution)/shard_map/psum | solution.py:76
  419.5 4.0 multiply_reduce_fusion.1
  423.5 5.1 multiply_convert_fusion.1
  428.7 4.5 copy.53
  433.2 5.2 reshape.159
  438.4 4.0 copy.54
  442.4 5.2 reshape.160
  447.6 24.5 %copy.63 = bf16[2,448,8,896]{3,2,1,0:T(8,128)(2,1)} copy(bf16[2,448,8,896]{1,0,3,2:T(2,128)(2,1)} %bitcast.16) | data formatting | bytes 25690112 | tf_op jit(solution)/shard_map/all_to_all | solution.py:82
  472.1 8.3 %fusion.52 = (bf16[1,8,448,896]{3,1,2,0:T(8,128)(2,1)}, bf16[1,8,448,896]{3,1,2,0:T(8,128)(2,1)S(1)}) fusion(bf16[2,8,448,896]{3,1,2,0:T(8,128)(2,1)} %bitcast.80), kind=kLoop, calls=%fused_computation.60 | loop fusion | bytes 25690112 | tf_op jit(solution)/shard_map/slice | solution.py:89
  480.4 3.9 copy.57
  488.1 5.9 fusion.54
  494.0 13.5 %convolution_convert_fusion.1 = bf16[384,3584]{1,0:T(8,128)(2,1)} fusion(bf16[896,3584]{1,0:T(8,128)(2,1)} %param.16, bf16[384,3584]{0,1:T(8,128)(2,1)} %reshape.160, bf16[3584,896]{1,0:T(8,128)(2,1)} %bitcast.83, f32[384,896]{1,0:T(8,128)} %fusion.54), kind=kOutput, calls=%fused_computation.15 | convolution fusion | flops 4937318400 | bytes 19726336 | tf_op jit(solution)/shard_map/dot_general | solution.py:92
  507.5 129.4 %all-reduce.5.cloned.1.call-done = bf16[384,3584]{1,0:T(8,128)(2,1)} async-done(((bf16[384,3584]{1,0:T(8,128)(2,1)}), bf16[384,3584]{1,0:T(8,128)(2,1)}) %all-reduce.5.cloned.1.call-update) | async-done | bytes 2752528 | tf_op jit(solution)/shard_map/psum | solution.py:76
  639.5 4.8 multiply_reduce_fusion
  644.3 8.0 %fusion.20 = bf16[384,1024]{1,0:T(8,128)(2,1)} fusion(bf16[3584,1024]{1,0:T(8,128)(2,1)} %param.17, f32[3584]{0:T(1024)S(1)} %copy-done.8, f32[384]{0:T(512)S(1)} %add_rsqrt_fusion, bf16[384,3584]{1,0:T(8,128)(2,1)S(1)} %copy-done.3, bf16[384,3584]{1,0:T(8,128)(2,1)S(1)} %copy-done, bf16[384,3584]{1,0:T(8,128)(2,1)S(1)} %copy-done.1, ...), kind=kOutput, calls=%fused_computation.34 | convolution fusion | flops 2835480576 | bytes 16431616 | tf_op jit(solution)/shard_map/dot_general | solution.py:95
  (45 shorter events, 20.2 us)
Async XLA Ops:
  6.5 79.8 %all-gather.8.cloned.1.call-start = ((), (), s32[]{:S(2)}) async-start(), calls=%async_computation.4 | async-start | bytes 13647872 | tf_op jit(solution)/shard_map/all_gather | solution.py:81
  9.4 135.8 %all-gather.4.cloned.1.call-start = ((), (), s32[]{:S(2)}) async-start(), calls=%async_computation.1 | async-start | bytes 3342336 | tf_op jit(solution)/shard_map/all_gather | solution.py:43
  11.3 156.6 %all-gather.6.cloned.1.call-start = ((), (), s32[]{:S(2)}) async-start(), calls=%async_computation.2 | async-start | bytes 3342336 | tf_op jit(solution)/shard_map/all_gather | solution.py:44
  134.9 312.7 %all-to-all-start = ((bf16[2,448,7168]{1,0,2:T(2,128)(2,1)}), bf16[2,448,7168]{1,0,2:T(2,128)(2,1)}, u32[]{:S(2)}, u32[]{:S(2)}) async-start(bf16[2,448,7168]{1,0,2:T(2,128)(2,1)} %copy.55), calls=%async_computation | async-start | bytes 29360128 | tf_op jit(solution)/shard_map/all_to_all | solution.py:82
  141.4 275.5 %all-reduce.3.cloned.1.call-start = ((), (), s32[]{:S(2)}) async-start(), calls=%async_computation.3 | async-start | bytes 5505024 | tf_op jit(solution)/shard_map/psum | solution.py:76
  150.7 6.5 copy-start.2
  167.9 13.2 %copy-start.4 = (bf16[512,3584]{1,0:T(8,128)(2,1)S(1)}, bf16[512,3584]{1,0:T(8,128)(2,1)}, u32[]{:S(2)}) copy-start(bf16[512,3584]{1,0:T(8,128)(2,1)} %param.14) | copy-start | bytes 11010052
  181.1 238.4 %copy-start.5 = (f32[3584]{0:T(1024)S(1)}, f32[3584]{0:T(1024)}, u32[]{:S(2)}) copy-start(f32[3584]{0:T(1024)} %param.18) | copy-start | bytes 43012
  184.3 239.2 %copy-start.6 = (f32[3584]{0:T(1024)S(1)}, f32[3584]{0:T(1024)}, u32[]{:S(2)}) copy-start(f32[3584]{0:T(1024)} %param.19) | copy-start | bytes 43012
  184.4 452.5 %all-reduce.5.cloned.1.call-start = ((), (), s32[]{:S(2)}) async-start(), calls=%async_computation.5 | async-start | bytes 5505024 | tf_op jit(solution)/shard_map/psum | solution.py:76
  416.9 6.6 copy-start
  507.4 132.0 %copy-start.7 = (f32[3584]{0:T(1024)S(1)}, f32[3584]{0:T(1024)}, u32[]{:S(2)}) copy-start(f32[3584]{0:T(1024)} %param.20) | copy-start | bytes 43012
  507.5 136.8 %copy-start.8 = (f32[3584]{0:T(1024)S(1)}, f32[3584]{0:T(1024)}, u32[]{:S(2)}) copy-start(f32[3584]{0:T(1024)} %param.21) | copy-start | bytes 43012
  636.9 7.4 %copy-start.1 = (bf16[384,3584]{1,0:T(8,128)(2,1)S(1)}, bf16[384,3584]{1,0:T(8,128)(2,1)}, u32[]{:S(2)}) copy-start(bf16[384,3584]{1,0:T(8,128)(2,1)} %param.11) | copy-start | bytes 8257540
  636.9 7.4 %copy-start.3 = (bf16[384,3584]{1,0:T(8,128)(2,1)S(1)}, bf16[384,3584]{1,0:T(8,128)(2,1)}, u32[]{:S(2)}) copy-start(bf16[384,3584]{1,0:T(8,128)(2,1)} %all-reduce.5.cloned.1.call-done) | copy-start | bytes 8257540
Sparse Core Ops, SparseCore 0:
  9.6 76.7 all-gather.7
  88.1 37.0 all-gather.3
  126.8 41.0 all-gather.5
  184.5 232.4 all-reduce.2
  507.6 129.2 all-reduce.4
where the time goes:
time: 662 us; the launch traced here: 659 us
  waiting for transfers between devices  439 us (66%)
  local copies, waits for them, and re-layouts  118 us (18%)
  matrix products  49.1 us (7%)
  other arithmetic  32.8 us (5%)
  between operations  13.3 us (2%)
  starting transfers between devices  6.85 us (1%)
    psum x2, waiting for transfers between devices, total_of(): return lax.psum(values.astype(jnp.bfloat16), 'tp').astype(jnp.float32)  362 us
    all_gather x1, waiting for transfers between devices, local(): stacked_rows = lax.all_gather(server_low, 'seq', axis=1, tiled=True)  72 us
    all_gather x1, local copies, waits for them, and re-layouts, local(): stacked_rows = lax.all_gather(server_low, 'seq', axis=1, tiled=True)  48.5 us
    all_to_all x1, local copies, waits for them, and re-layouts, local(): lax.all_to_all(stacked_rows, 'tp', split_axis=2, concat_axis=1, tiled=True)  24.5 us
    reduce_sum x4, other arithmetic, rms_norm(): meansq = jnp.mean(values * values, axis=-1, keepdims=True)  13.9 us
    dot_general x1, matrix products, local(): jnp.dot(activated, down_weight, preferred_element_type=jnp.float32)  13.5 us
  transfers between devices with their start and end apart: 6, of which 4 were waited for; matrix products, arithmetic and copies ran while one was open for 17% of the time, Pallas kernels for 0%

commit v1 on v0

--- a/solution.py
+++ b/solution.py
@@ -26,10 +26,8 @@
     post_ffw_gain,
     next_gain,
 ):
-    seq_count = lax.axis_size("seq")
     tp_count = lax.axis_size("tp")
     row_count = hidden_in.shape[0]
-    model_width = hidden_in.shape[1]
     per_group = HEADS // KV_HEADS
     group_cols = (per_group + 2) * HEAD_DIM
     local_groups = joined_inputs.shape[1] // group_cols
@@ -72,26 +70,28 @@
     attended = blended.astype(jnp.bfloat16).reshape(row_count, local_groups * per_group * HEAD_DIM)
     projected = jnp.dot(attended, o_weight, preferred_element_type=jnp.float32)
 
-    def total_of(values):
-        return lax.psum(values.astype(jnp.bfloat16), "tp").astype(jnp.float32)
+    tp_index = lax.axis_index("tp")
+    slice_rows = row_count // tp_count
 
-    residual_mid = hidden_in.astype(jnp.float32) + rms_norm(total_of(projected), post_attn_gain)
+    def scattered(values):
+        return lax.psum_scatter(
+            values.astype(jnp.bfloat16), "tp", scatter_dimension=0, tiled=True
+        ).astype(jnp.float32)
+
+    own_hidden = lax.dynamic_slice_in_dim(hidden_in, tp_index * slice_rows, slice_rows, 0)
+    residual_mid = own_hidden.astype(jnp.float32) + rms_norm(scattered(projected), post_attn_gain)
     ffw_in = rms_norm(residual_mid, pre_ffw_gain).astype(jnp.bfloat16)
+    ffw_in = lax.all_gather(ffw_in, "tp", axis=0, tiled=True)
     server_low = gate_up.astype(jnp.bfloat16)
-    stacked_rows = lax.all_gather(server_low, "seq", axis=1, tiled=True)
-    local_units = lax.all_to_all(stacked_rows, "tp", split_axis=2, concat_axis=1, tiled=True)
-    piece_rows = gate_up.shape[1]
-    reordered = (
-        ffw_in.reshape(row_count, seq_count, tp_count, piece_rows)
-        .transpose(0, 2, 1, 3)
-        .reshape(row_count, model_width)
-    )
-    gate = jnp.dot(reordered, local_units[0], preferred_element_type=jnp.float32)
-    up_part = jnp.dot(reordered, local_units[1], preferred_element_type=jnp.float32)
+    unit_rows = lax.all_to_all(server_low, "tp", split_axis=2, concat_axis=1, tiled=True)
+    local_units = lax.all_gather(unit_rows, "seq", axis=1, tiled=True)
+    gate = jnp.dot(ffw_in, local_units[0], preferred_element_type=jnp.float32)
+    up_part = jnp.dot(ffw_in, local_units[1], preferred_element_type=jnp.float32)
     activated = (jax.nn.gelu(gate, approximate=True) * up_part).astype(jnp.bfloat16)
     ffw_out = jnp.dot(activated, down_weight, preferred_element_type=jnp.float32)
-    residual_out = residual_mid + rms_norm(total_of(ffw_out), post_ffw_gain)
+    residual_out = residual_mid + rms_norm(scattered(ffw_out), post_ffw_gain)
     next_in = rms_norm(residual_out, next_gain).astype(jnp.bfloat16)
+    next_in = lax.all_gather(next_in, "tp", axis=0, tiled=True)
     return jnp.dot(next_in, next_weight, preferred_element_type=jnp.float32).astype(jnp.bfloat16)
 
 

time: 662 us -> 498 us (0.75)
  waiting for transfers between devices: 439 us -> 317 us
  local copies, waits for them, and re-layouts: 118 us -> 71 us
  blocking collectives: 0 us -> 21.5 us
  other arithmetic: 32.8 us -> 19.9 us
    psum x2 -> x0, waiting for transfers between devices: 362 us -> none  [total_of(): return lax.psum(values.astype(jnp.bfloat16), 'tp').astype(jnp.float32)]
    reduce_scatter x0 -> x2, waiting for transfers between devices: none -> 96.9 us  [scattered(): lax.psum_scatter(values.astype(jnp.bfloat16), 'tp', scatter_dimension=0,...]
    all_gather x1 -> x3, waiting for transfers between devices: 72 us -> 166 us  [the longest x1 70.7 us: local(): local_units = lax.all_gather(unit_rows, 'seq', axis=1, tiled=True)]
    all_gather x1 -> x0, local copies, waits for them, and re-layouts: 48.5 us -> none  [local(): stacked_rows = lax.all_gather(server_low, 'seq', axis=1, tiled=True)]
    all_gather x1, waiting for transfers between devices: 0.01 us -> 33.6 us  [local(): lax.all_gather(own_keys, 'seq', axis=0, tiled=True)]
    all_to_all x0 -> x1, blocking collectives: none -> 21.5 us  [local(): lax.all_to_all(server_low, 'tp', split_axis=2, concat_axis=1, tiled=True)]
    unnamed x18 -> x21, local copies, waits for them, and re-layouts: 6.5 us -> 25.8 us
    all_gather x1, waiting for transfers between devices: 4.66 us -> 19.7 us  [local(): lax.all_gather(own_values, 'seq', axis=0, tiled=True)]
  transfers between devices with their start and end apart: 6 -> 7, of which waited for: 4 -> 7; matrix products, arithmetic and copies ran while one was open for 17% -> 17% of each run, Pallas kernels for 0% -> 0%
where the time goes in v1:
time: 498 us
  waiting for transfers between devices  317 us (64%)
  local copies, waits for them, and re-layouts  71 us (14%)
  matrix products  54.3 us (11%)
  blocking collectives  21.5 us (4%)
  other arithmetic  19.9 us (4%)
  between operations  13.7 us (3%)
    reduce_scatter x2, waiting for transfers between devices, scattered(): lax.psum_scatter(values.astype(jnp.bfloat16), 'tp', scatter_dimension=0,...  96.9 us
    all_gather x1, waiting for transfers between devices, local(): local_units = lax.all_gather(unit_rows, 'seq', axis=1, tiled=True)  70.7 us
    all_gather x1, waiting for transfers between devices, local(): next_in = lax.all_gather(next_in, 'tp', axis=0, tiled=True)  59.3 us
    all_gather x1, waiting for transfers between devices, local(): ffw_in = lax.all_gather(ffw_in, 'tp', axis=0, tiled=True)  35.7 us
    all_gather x1, waiting for transfers between devices, local(): lax.all_gather(own_keys, 'seq', axis=0, tiled=True)  33.6 us
    slice x1, local copies, waits for them, and re-layouts, local(): gate = jnp.dot(ffw_in, local_units[0], preferred_element_type=jnp.float32)  26 us
    unnamed x21, local copies, waits for them, and re-layouts  25.8 us
    all_to_all x1, blocking collectives, local(): lax.all_to_all(server_low, 'tp', split_axis=2, concat_axis=1, tiled=True)  21.5 us
  transfers between devices with their start and end apart: 7, of which 7 were waited for; matrix products, arithmetic and copies ran while one was open for 17% of the time, Pallas kernels for 0%

profile of v1, /device:TPU:1, one launch (start us, length us, event | category | flops | bytes accessed | tf_op | source)
XLA Modules:
  0.0 497.7 jit_solution(12675945497495161882)
XLA Ops:
  11.5 3.8 fusion.6
  15.2 33.6 %all-gather.6.cloned.1.call-done = bf16[6144,1,256]{2,0,1:T(8,128)(2,1)} async-done(((bf16[384,1,256]{2,0,1:T(8,128)(2,1)}), bf16[6144,1,256]{2,0,1:T(8,128)(2,1)}) %all-gather.6.cloned.1.call-update) | async-done | bytes 3145744 | tf_op jit(solution)/shard_map/all_gather | solution.py:41
  48.8 5.4 %fusion = (f32[384,2]{0,1:T(2,128)S(1)}, f32[6144,384,2]{1,0,2:T(8,128)S(1)}) fusion(pred[384,6144]{0,1:T(8,128)(4,1)} %fusion.6, bf16[384,2,256]{0,2,1:T(8,128)(2,1)S(1)} %bitcast.100, bf16[6144,1,256]{2,0,1:T(8,128)(2,1)} %all-gather.6.cloned.1.call-done), kind=kOutput, calls=%fused_computation.2 | convolution fusion | flops 2430074112 | bytes 24775680 | tf_op jit(solution)/shard_map/qgrd,kgd->qgrk/dot_general | solution.py:54
  54.2 6.4 %copy-done = f32[6144,384,2]{1,0,2:T(8,128)} copy-done((f32[6144,384,2]{1,0,2:T(8,128)}, f32[6144,384,2]{1,0,2:T(8,128)S(1)}, u32[]{:S(2)}) %copy-start) | copy-done | bytes 18874392
  60.6 6.1 %fusion.1 = f32[384,2]{0,1:T(2,128)S(1)} fusion(f32[6144,384,2]{1,0,2:T(8,128)S(1)} %get-tuple-element.10, f32[384,2]{0,1:T(2,128)S(1)} %get-tuple-element.9, pred[384,6144]{0,1:T(8,128)(4,1)} %fusion.6), kind=kLoop, calls=%fused_computation.3 | loop fusion | flops 23592192 | bytes 21239808 | tf_op jit(solution)/shard_map/reduce_sum | solution.py:62
  66.8 19.7 %all-gather.8.cloned.1.call-done = bf16[6144,1,256]{2,0,1:T(8,128)(2,1)} async-done(((bf16[384,1,256]{2,0,1:T(8,128)(2,1)}), bf16[6144,1,256]{2,0,1:T(8,128)(2,1)}) %all-gather.8.cloned.1.call-update) | async-done | bytes 3145744 | tf_op jit(solution)/shard_map/all_gather | solution.py:42
  86.5 13.2 %fusion.32 = bf16[1,256,384,2]{2,1,3,0:T(8,128)(2,1)S(1)} fusion(bf16[6144,1,256]{2,0,1:T(8,128)(2,1)} %all-gather.8.cloned.1.call-done, f32[6144,384,2]{1,0,2:T(8,128)} %copy-done, f32[384,2]{0,1:T(2,128)S(1)} %get-tuple-element.9, pred[384,6144]{0,1:T(8,128)(4,1)} %fusion.6, f32[384,2]{0,1:T(2,128)S(1)} %fusion.1), kind=kOutput, calls=%fused_computation.33 | convolution fusion | flops 2439905280 | bytes 24778752 | tf_op jit(solution)/shard_map/qgrk,kgd->qgrd/dot_general | solution.py:63
  99.7 3.2 convolution_convert_fusion
  103.6 6.2 %copy.53 = bf16[2,28,7168]{1,0,2:T(2,128)(2,1)} copy(bf16[2,28,7168]{2,1,0:T(8,128)(2,1)S(1)} %copy.72) | data formatting | bytes 1605632 | tf_op jit(solution)/shard_map/convert_element_type | solution.py:85
  109.8 8.3 %reshape.151 = bf16[8,2,25088]{2,1,0:T(2,128)(2,1)S(1)} reshape(bf16[7168,2,28]{2,1,0:T(2,128)(2,1)} %bitcast.95) | data formatting | bytes 1605632
  118.0 21.5 %all_to_all.18 = bf16[8,2,25088]{2,1,0:T(2,128)(2,1)S(1)} all-to-all(bf16[8,2,25088]{2,1,0:T(2,128)(2,1)S(1)} %reshape.151), channel_id=1, replica_groups=mesh['seq'=16,'tp'=8] {'tp'}, dimensions={0} | all-to-all | bytes 1605632 | tf_op jit(solution)/shard_map/all_to_all | solution.py:86
  139.5 10.6 %reshape.152 = bf16[7168,2,28]{2,1,0:T(2,128)(2,1)} reshape(bf16[8,2,25088]{2,1,0:T(2,128)(2,1)S(1)} %all_to_all.18) | data formatting | bytes 1605632
  150.1 9.9 %copy.54 = bf16[2,28,8,896]{3,0,1,2:T(2,128)(2,1)} copy(bf16[2,28,8,896]{1,0,3,2:T(2,128)(2,1)} %bitcast.96) | data formatting | bytes 1605632 | tf_op jit(solution)/shard_map/all_to_all | solution.py:86
  160.1 22.6 %reduce-scatter.3.cloned.1.call-done = bf16[48,3584]{1,0:T(8,128)(2,1)} async-done(((bf16[384,3584]{1,0:T(8,128)(2,1)}), bf16[48,3584]{1,0:T(8,128)(2,1)}) %reduce-scatter.3.cloned.1.call-update) | async-done | bytes 344080 | tf_op jit(solution)/shard_map/reduce_scatter | solution.py:77
  185.2 1.9 multiply_convert_fusion.1
  187.2 70.7 %all-gather.12.cloned.1.call-done = bf16[2,3584,896]{2,0,1:T(2,128)(2,1)} async-done(((bf16[2,224,896]{2,0,1:T(2,128)(2,1)}), bf16[2,3584,896]{2,0,1:T(2,128)(2,1)}) %all-gather.12.cloned.1.call-update) | async-done | bytes 12845072 | tf_op jit(solution)/shard_map/all_gather | solution.py:87
  258.0 26.0 %fusion.46 = (bf16[1,3584,896]{2,0,1:T(2,128)(2,1)}, bf16[1,3584,896]{2,0,1:T(2,128)(2,1)}) fusion(bf16[2,3584,896]{2,0,1:T(2,128)(2,1)} %all-gather.12.cloned.1.call-done), kind=kLoop, calls=%fused_computation.58 | loop fusion | bytes 25690112 | tf_op jit(solution)/shard_map/slice | solution.py:88
  284.0 35.7 %all-gather.10.cloned.1.call-done = bf16[384,3584]{1,0:T(8,128)(2,1)} async-done(((bf16[48,3584]{1,0:T(8,128)(2,1)}), bf16[384,3584]{1,0:T(8,128)(2,1)}) %all-gather.10.cloned.1.call-update) | async-done | bytes 2752528 | tf_op jit(solution)/shard_map/all_gather | solution.py:84
  319.7 9.6 %fusion.9 = f32[384,896]{1,0:T(8,128)} fusion(bf16[384,3584]{1,0:T(8,128)(2,1)} %all-gather.10.cloned.1.call-done, bf16[1,3584,896]{2,0,1:T(2,128)(2,1)} %get-tuple-element.5), kind=kOutput, calls=%fused_computation.13 | convolution fusion | flops 2466250752 | bytes 10551296 | tf_op jit(solution)/shard_map/dot_general | solution.py:88
  329.3 15.2 %convolution_convert_fusion.1 = bf16[384,3584]{1,0:T(8,128)(2,1)} fusion(bf16[896,3584]{1,0:T(8,128)(2,1)} %param.16, bf16[384,3584]{1,0:T(8,128)(2,1)} %all-gather.10.cloned.1.call-done, bf16[1,3584,896]{2,0,1:T(2,128)(2,1)} %get-tuple-element.6, f32[384,896]{1,0:T(8,128)} %fusion.9), kind=kOutput, calls=%fused_computation.15 | convolution fusion | flops 4937318400 | bytes 19726336 | tf_op jit(solution)/shard_map/dot_general | solution.py:91
  344.8 74.3 %reduce-scatter.5.cloned.1.call-done = bf16[48,3584]{1,0:T(8,128)(2,1)} async-done(((bf16[384,3584]{1,0:T(8,128)(2,1)}), bf16[48,3584]{1,0:T(8,128)(2,1)}) %reduce-scatter.5.cloned.1.call-update) | async-done | bytes 344080 | tf_op jit(solution)/shard_map/reduce_scatter | solution.py:77
  421.7 2.0 multiply_convert_fusion
  423.8 59.3 %all-gather.14.cloned.1.call-done = bf16[384,3584]{1,0:T(8,128)(2,1)} async-done(((bf16[48,3584]{1,0:T(8,128)(2,1)}), bf16[384,3584]{1,0:T(8,128)(2,1)}) %all-gather.14.cloned.1.call-update) | async-done | bytes 2752528 | tf_op jit(solution)/shard_map/all_gather | solution.py:94
  483.1 7.8 %convolution_convert_fusion.2 = bf16[384,1024]{1,0:T(8,128)(2,1)} fusion(bf16[384,3584]{1,0:T(8,128)(2,1)} %all-gather.14.cloned.1.call-done, bf16[3584,1024]{1,0:T(8,128)(2,1)} %param.17), kind=kOutput, calls=%fused_computation.22 | convolution fusion | flops 2818965504 | bytes 10878976 | tf_op jit(solution)/shard_map/dot_general | solution.py:95
  (47 shorter events, 11.0 us)
Async XLA Ops:
  6.5 42.2 %all-gather.6.cloned.1.call-start = ((), (), s32[]{:S(2)}) async-start(), calls=%async_computation.3 | async-start | bytes 3342336 | tf_op jit(solution)/shard_map/all_gather | solution.py:41
  8.3 78.1 %all-gather.8.cloned.1.call-start = ((), (), s32[]{:S(2)}) async-start(), calls=%async_computation.4 | async-start | bytes 3342336 | tf_op jit(solution)/shard_map/all_gather | solution.py:42
  9.1 173.6 %reduce-scatter.3.cloned.1.call-start = ((), (), s32[]{:S(2)}) async-start(), calls=%async_computation.5 | async-start | bytes 3096576 | tf_op jit(solution)/shard_map/reduce_scatter | solution.py:77
  54.2 6.5 %copy-start = (f32[6144,384,2]{1,0,2:T(8,128)}, f32[6144,384,2]{1,0,2:T(8,128)S(1)}, u32[]{:S(2)}) copy-start(f32[6144,384,2]{1,0,2:T(8,128)S(1)} %get-tuple-element.10) | copy-start | bytes 56623108
  86.5 13.2 %copy-start.2 = (bf16[512,3584]{1,0:T(8,128)(2,1)S(1)}, bf16[512,3584]{1,0:T(8,128)(2,1)}, u32[]{:S(2)}) copy-start(bf16[512,3584]{1,0:T(8,128)(2,1)} %param.14) | copy-start | bytes 11010052
  99.7 3.4 copy-start.3
  102.9 155.1 %all-gather.12.cloned.1.call-start = ((), (), s32[]{:S(2)}) async-start(), calls=%async_computation.7 | async-start | bytes 13647872 | tf_op jit(solution)/shard_map/all_gather | solution.py:87
  150.1 33.8 %copy-start.4 = (bf16[384,3584]{1,0:T(8,128)(2,1)S(1)}, bf16[384,3584]{1,0:T(8,128)(2,1)}, u32[]{:S(2)}) copy-start(bf16[384,3584]{1,0:T(8,128)(2,1)} %param.11) | copy-start | bytes 8257540
  150.1 33.8 %copy-start.5 = (f32[3584]{0:T(1024)S(1)}, f32[3584]{0:T(1024)}, u32[]{:S(2)}) copy-start(f32[3584]{0:T(1024)} %param.18) | copy-start | bytes 43012
  150.1 35.1 %copy-start.7 = (f32[3584]{0:T(1024)S(1)}, f32[3584]{0:T(1024)}, u32[]{:S(2)}) copy-start(f32[3584]{0:T(1024)} %param.19) | copy-start | bytes 43012
  160.0 159.7 %all-gather.10.cloned.1.call-start = ((), (), s32[]{:S(2)}) async-start(), calls=%async_computation.6 | async-start | bytes 3096576 | tf_op jit(solution)/shard_map/all_gather | solution.py:84
  187.2 231.9 %reduce-scatter.5.cloned.1.call-start = ((), (), s32[]{:S(2)}) async-start(), calls=%async_computation.8 | async-start | bytes 3096576 | tf_op jit(solution)/shard_map/reduce_scatter | solution.py:77
  329.3 91.0 %copy-start.1 = (bf16[48,3584]{1,0:T(8,128)(2,1)S(1)}, bf16[48,3584]{1,0:T(8,128)(2,1)}, u32[]{:S(2)}) copy-start(bf16[48,3584]{1,0:T(8,128)(2,1)} %reduce-scatter.3.cloned.1.call-done) | copy-start | bytes 1032196
  329.3 91.0 %copy-start.6 = (f32[3584]{0:T(1024)S(1)}, f32[3584]{0:T(1024)}, u32[]{:S(2)}) copy-start(f32[3584]{0:T(1024)} %param.20) | copy-start | bytes 43012
  344.5 77.2 %copy-start.8 = (f32[3584]{0:T(1024)S(1)}, f32[3584]{0:T(1024)}, u32[]{:S(2)}) copy-start(f32[3584]{0:T(1024)} %param.21) | copy-start | bytes 43012
  344.5 138.5 %all-gather.14.cloned.1.call-start = ((), (), s32[]{:S(2)}) async-start(), calls=%async_computation.9 | async-start | bytes 3096576 | tf_op jit(solution)/shard_map/all_gather | solution.py:94
Sparse Core Ops, SparseCore 0:
  9.1 39.6 all-gather.5
  50.5 35.9 all-gather.7
  103.0 79.6 reduce-scatter.2
  184.3 73.6 all-gather.11
  260.1 59.5 all-gather.9
  344.6 74.4 reduce-scatter.4
  423.9 59.1 all-gather.13

commit v2 on v1

v2 whole, which is shorter than its diff:
```python
import jax
import jax.numpy as jnp
from jax import lax
from jax.experimental import pallas as pl
from jax.experimental.pallas import tpu as pltpu
from jax.sharding import PartitionSpec as P

MESH = pl.DeviceIdType.MESH
BF = jnp.bfloat16
F32 = jnp.float32
D = 3584
HALF = D // 2
ROWS = 384
HD = 256
UNITS = 896
PIECE = 28
CHUNK = 224
BLK = 48
GROUP = 192
QKV = 1024
NEG = -1e30


def al(value, to):
    return pl.multiple_of(value, to)


def kernel(
    lens, hid, joined, ow, gu, dw, nw, g_attn, g_pre, g_post, g_next,
    out,
    qbuf, kvbuf, owv, dwv, nwv, hidv, guv, gub, abuf, wbuf,
    mbuf, lbuf, acc, att, pb1, pb2, r1, r2, rx, sx, ag1, ag2, act, resid,
    lsem, kv_s, kv_r, a_s, a_r, w_s, w_r, r1_r, r2_r, rx_r, rs_s, ag_s, ag_r,
):
    s = lax.axis_index("seq")
    t = lax.axis_index("tp")
    x = s // 8
    z = (s // 2) % 4
    c = s % 2
    y = t // 2
    h = t % 2
    o = 1 - h

    def dev_seq(xx, zz, cc):
        return (xx * 8 + zz * 2 + cc, t)

    def dev_tp(yy, hh):
        return (s, yy * 2 + hh)

    zp, zm = (z + 1) % 4, (z + 3) % 4
    yp, ym, y2 = (y + 1) % 4, (y + 3) % 4, (y + 2) % 4
    sib = dev_seq(x, z, 1 - c)
    xnb = dev_seq(1 - x, z, c)
    zup = dev_seq(x, zp, c)
    zdn = dev_seq(x, zm, c)
    yup = dev_tp(yp, h)
    ydn = dev_tp(ym, h)
    xhi = dev_tp(y, o)

    barrier = pltpu.get_barrier_semaphore()
    tp_peers = [(s, (t + k) % 8) for k in range(1, 8)]
    for peer in [sib, xnb, zup, zdn] + tp_peers:
        pl.semaphore_signal(barrier, inc=1, device_id=peer, device_id_type=MESH)

    own_block = h * 4 + y
    loads = [
        (joined.at[:, pl.ds(512, 512)], kvbuf.at[s]),
        (joined.at[:, pl.ds(0, 256)], qbuf.at[0]),
        (joined.at[:, pl.ds(256, 256)], qbuf.at[1]),
        (gu, guv),
        (ow, owv),
        (hid.at[pl.ds(al(own_block * BLK, 16), BLK), :], hidv),
        (dw, dwv),
        (nw, nwv),
    ]
    local_copies = [
        pltpu.make_async_copy(src, dst, lsem.at[i]) for i, (src, dst) in enumerate(loads)
    ]
    for copy in local_copies:
        copy.start()

    def rcopy(src, dst, send, recv, dev):
        return pltpu.make_async_remote_copy(
            src_ref=src,
            dst_ref=dst,
            send_sem=send,
            recv_sem=recv,
            device_id=dev,
            device_id_type=MESH,
        )

    pl.semaphore_wait(barrier, 11)

    def kv_send(slot, dev, sem):
        return rcopy(kvbuf.at[slot], kvbuf.at[slot], kv_s.at[sem], kv_r.at[slot], dev)

    def kv_arrived(slot):
        kv_send(slot, sib, 0).wait_recv()

    kv_sent = []

    def kv_go(cond, slot, dev):
        sem = len(kv_sent)
        kv_sent.append((cond, slot, dev))

        @pl.when(cond)
        def _():
            kv_send(slot, dev, sem).start()

    local_copies[0].wait()
    always = s >= 0
    kv_go(z < 3, s, zup)
    kv_go(x == 0, s, xnb)
    kv_go(z == 0, s, zdn)
    kv_go(c == 0, s, sib)

    local_copies[3].wait()
    for k in range(8):
        gub[k] = guv[:, :, k * UNITS : (k + 1) * UNITS].astype(BF)

    def a_send(k):
        peer = (t + k) % 8
        return rcopy(gub.at[peer], abuf.at[t], a_s.at[k], a_r.at[k], (s, peer))

    for k in range(1, 8):
        a_send(k).start()

    local_copies[1].wait()
    local_copies[2].wait()
    mbuf[...] = jnp.full(mbuf.shape, NEG, F32)
    lbuf[...] = jnp.zeros(lbuf.shape, F32)
    acc[...] = jnp.zeros(acc.shape, F32)

    end0 = lens[0]
    end1 = end0 + lens[1]
    end2 = end1 + lens[2]

    def flash(slot):
        place = s * ROWS + lax.broadcasted_iota(jnp.int32, (ROWS, 1), 0)
        low = jnp.where(
            place >= end2,
            end2,
            jnp.where(place >= end1, end1, jnp.where(place >= end0, end0, 0)),
        )
        other = slot * ROWS + lax.broadcasted_iota(jnp.int32, (ROWS, ROWS), 1)
        allowed = (other >= low) & (other <= place)

        def head(r, carry):
            scores = lax.dot_general(
                qbuf[r],
                kvbuf[slot, :, 0:HD],
                (((1,), (1,)), ((), ())),
                preferred_element_type=F32,
            ) * (HD ** -0.5)
            scores = jnp.where(allowed, scores, NEG)
            before = mbuf[r]
            peak = jnp.maximum(before, jnp.max(scores, axis=-1, keepdims=True))
            weights = jnp.exp(scores - peak)
            fade = jnp.exp(before - peak)
            lbuf[r] = lbuf[r] * fade + jnp.sum(weights, axis=-1, keepdims=True)
            mbuf[r] = peak
            acc[r] = acc[r] * fade + jnp.dot(
                weights.astype(BF), kvbuf[slot, :, HD : 2 * HD], preferred_element_type=F32
            )
            return carry

        lax.fori_loop(0, 2, head, 0)

    def up_ok(off):
        return z + off >= 0

    def down_ok(off):
        return (x == 1) & (z + off <= 3)

    def up_slot(off, core):
        return x * 8 + (z + off + 4) % 4 * 2 + core

    def down_slot(off, core):
        return (z + off) % 4 * 2 + core

    def w_ref(slot, m):
        return wbuf.at[m, pl.ds(al(slot * CHUNK, 16), CHUNK), :]

    w_sent = []

    def w_copy(slot, m, dev, sem):
        return rcopy(w_ref(slot, m), w_ref(slot, m), w_s.at[sem], w_r.at[slot, m], dev)

    def w_go(slot, m, dev):
        w_copy(slot, m, dev, len(w_sent)).start()
        w_sent.append((slot, m, dev))

    def w_arrived(slot, m):
        w_copy(slot, m, sib, 0).wait_recv()

    def repack():
        for k in range(1, 8):
            peer = (t + 8 - k) % 8
            rcopy(gub.at[0], abuf.at[peer], a_s.at[k], a_r.at[k], (s, peer)).wait_recv()
        abuf[t] = gub[t]
        for m in range(2):
            rows = jnp.concatenate([abuf[k, m].astype(F32) for k in range(8)], axis=0)
            wbuf[m, pl.ds(al(s * CHUNK, 16), CHUNK), :] = rows.astype(BF)

    def comm_of(entries):
        plan = []
        for cond, slot, forward, relays in entries:
            sends = [(cond if forward is None else cond & forward, sib)] + relays
            numbered = []
            for ok, dev in sends:
                numbered.append((ok, dev, len(kv_sent)))
                kv_sent.append((ok, slot, dev))
            plan.append((cond, slot, numbered))

        def run():
            for cond, slot, numbered in plan:

                @pl.when(cond)
                def _(slot=slot):
                    kv_arrived(slot)

                for ok, dev, sem in numbered[1:] + numbered[:1]:

                    @pl.when(ok)
                    def _(slot=slot, dev=dev, sem=sem):
                        kv_send(slot, dev, sem).start()

        return run

    middle = (z == 1) | (z == 2)
    comm_a = comm_of([
        (up_ok(-1), up_slot(-1, c), None, [(middle, zup)]),
        (down_ok(0), down_slot(0, c), c == 1, [((x == 1) & (z >= 1), zdn), ((x == 1) & (z == 3), zup)]),
    ])
    comm_b = comm_of([
        (down_ok(1), down_slot(1, c), None, [((x == 1) & middle, zdn)]),
        (up_ok(-3), up_slot(-3, c), None, []),
        (down_ok(3), down_slot(3, c), None, []),
    ])
    comm_c = comm_of([
        (up_ok(-2), up_slot(-2, c), None, []),
        (down_ok(2), down_slot(2, c), None, []),
    ])

    offsets = {2: -1, 3: 0, 4: -1, 5: 0, 6: 1, 7: -3, 8: 3, 9: 1, 10: -3, 11: 3, 12: -2, 13: 2, 14: -2, 15: 2}

    def step(i, carry):
        @pl.when(i == 2)
        def _():
            comm_a()

        @pl.when(i == 6)
        def _():
            comm_b()

        @pl.when(i == 12)
        def _():
            comm_c()

        off = 0
        for k, value in offsets.items():
            off = off + jnp.where(i == k, value, 0)
        from_sib = (i == 1) | (i == 4) | (i == 5) | ((i >= 9) & (i <= 11)) | (i >= 14)
        is_down = (i >= 2) & (off >= 0)
        column = jnp.where(is_down, 0, x)
        zz = z + off
        ok = jnp.where(is_down, (x == 1) & (zz <= 3), zz >= 0)
        ok = ok & ((i != 1) | (c == 1)) & ((i != 5) | (c == 0))
        core = jnp.where(from_sib, 1 - c, c)
        slot = column * 8 + (zz + 4) % 4 * 2 + core

        @pl.when(ok & from_sib)
        def _():
            kv_arrived(slot)

        @pl.when(ok)
        def _():
            flash(slot)

        return carry

    lax.fori_loop(0, 16, step, 0)

    repack()
    for r in range(2):
        att[:, r * HD : (r + 1) * HD] = (acc[r] / lbuf[r, :, 0:1]).astype(BF)

    for m in range(2):
        w_go(s, m, xnb)
    w_go(s, 0, zup)
    w_go(s, 1, zdn)
    w_go(s, 1, zup)
    w_go(s, 0, zdn)
    for m in range(2):
        w_go(s, m, sib)

    s_x = (1 - x) * 8 + z * 2 + c
    s_zm = x * 8 + zm * 2 + c
    s_zp = x * 8 + zp * 2 + c
    s_z2 = x * 8 + (z + 2) % 4 * 2 + c
    s_xzm = (1 - x) * 8 + zm * 2 + c
    s_xzp = (1 - x) * 8 + zp * 2 + c
    s_xz2 = (1 - x) * 8 + (z + 2) % 4 * 2 + c

    def w_stage1():
        w_arrived(s_zm, 0)
        w_go(s_zm, 0, zup)
        w_arrived(s_zp, 1)
        w_go(s_zp, 1, zdn)
        for m in range(2):
            w_arrived(s_x, m)
        w_go(s_x, 0, zup)
        w_go(s_x, 1, zdn)
        w_go(s_x, 1, zup)
        w_go(s_x, 0, zdn)
        w_arrived(s_zm, 1)
        w_arrived(s_zp, 0)
        for slot in (s_x, s_zm, s_zp):
            for m in range(2):
                w_go(slot, m, sib)

    def w_stage2():
        for m in range(2):
            w_arrived(s_z2, m)
            w_go(s_z2, m, xnb)
            w_go(s_z2, m, sib)

    def w_stage3():
        for slot in (s_xzm, s_xzp):
            for m in range(2):
                w_arrived(slot, m)
                w_go(slot, m, sib)

    def w_stage4():
        for m in range(2):
            w_arrived(s_xz2, m)
            w_go(s_xz2, m, sib)

    def w_stage5():
        for xx in range(2):
            for zz in range(4):
                for m in range(2):
                    w_arrived(xx * 8 + zz * 2 + 1 - c, m)

    rs_sent = []

    def send(src, dst, recv, dev):
        copy = rcopy(src, dst, rs_s.at[len(rs_sent)], recv, dev)
        copy.start()
        rs_sent.append(copy)

    def rows_of(block):
        return pl.ds(al(block * BLK, 16), BLK)

    cols = (pl.ds(0, HALF), pl.ds(HALF, HALF))
    phase_h = (o, h)

    def rs_start(k, pb, p):
        g = phase_h[p]
        far = rows_of(g * 4 + y2)
        send(pb.at[far, cols[0]], r1.at[k, p, 0], r1_r.at[k, p, 0], yup)
        send(pb.at[far, cols[1]], r1.at[k, p, 1], r1_r.at[k, p, 1], ydn)
        send(pb.at[rows_of(g * 4 + yp), cols[1]], r2.at[k, p, 0, 1], r2_r.at[k, p, 0, 1], yup)
        send(pb.at[rows_of(g * 4 + ym), cols[0]], r2.at[k, p, 1, 0], r2_r.at[k, p, 1, 0], ydn)

    def rs_middle(k, pb, p):
        g = phase_h[p]
        for way, (yy, dev) in enumerate(((yp, yup), (ym, ydn))):
            near = rows_of(g * 4 + yy)
            rcopy(r1.at[k, p, way], r1.at[k, p, way], rs_s.at[0], r1_r.at[k, p, way], dev).wait_recv()
            pb[near, cols[way]] = (
                pb[near, cols[way]].astype(F32) + r1[k, p, way].astype(F32)
            ).astype(BF)
            send(pb.at[near, cols[way]], r2.at[k, p, way, way], r2_r.at[k, p, way, way], dev)

    def rs_end(k, pb, p):
        g = phase_h[p]
        for way in range(2):
            for half in range(2):
                ref = r2.at[k, p, way, half]
                rcopy(ref, ref, rs_s.at[0], r2_r.at[k, p, way, half], yup).wait_recv()
        mine = rows_of(g * 4 + y)
        return jnp.concatenate(
            [
                pb[mine, cols[half]].astype(F32)
                + r2[k, p, 0, half].astype(F32)
                + r2[k, p, 1, half].astype(F32)
                for half in range(2)
            ],
            axis=1,
        )

    def rs_cross(k, pb):
        sx[k] = rs_end(k, pb, 0).astype(BF)
        send(sx.at[k], rx.at[k], rx_r.at[k], xhi)

    def rs_total(k, pb):
        total = rs_end(k, pb, 1)
        rcopy(rx.at[k], rx.at[k], rs_s.at[0], rx_r.at[k], xhi).wait_recv()
        return total + rx[k].astype(F32)

    def normed(values, gain):
        meansq = jnp.mean(values * values, axis=-1, keepdims=True)
        return values * lax.rsqrt(meansq + 1e-06) * gain[...]

    ag_sent = []

    def ag_copy(k, ag, block, half, dev, sem):
        ref = ag.at[rows_of(block), cols[half]]
        return rcopy(ref, ref, ag_s.at[sem], ag_r.at[k, block, half], dev)

    def ag_go(k, ag, block, half, dev):
        copy = ag_copy(k, ag, block, half, dev, len(ag_sent))
        copy.start()
        ag_sent.append(copy)

    def ag_arrived(k, ag, block, half):
        ag_copy(k, ag, block, half, xhi, 0).wait_recv()

    def ag_start(k, ag):
        b = h * 4 + y
        ag_go(k, ag, b, 0, xhi)
        ag_go(k, ag, b, 1, xhi)
        ag_go(k, ag, b, 0, yup)
        ag_go(k, ag, b, 1, ydn)
        ag_go(k, ag, b, 1, yup)
        ag_go(k, ag, b, 0, ydn)

    def ag_relay(k, ag, g):
        ag_arrived(k, ag, g * 4 + ym, 0)
        ag_go(k, ag, g * 4 + ym, 0, yup)
        ag_arrived(k, ag, g * 4 + yp, 1)
        ag_go(k, ag, g * 4 + yp, 1, ydn)

    def ag_cross(k, ag):
        b = o * 4 + y
        for half in range(2):
            ag_arrived(k, ag, b, half)
        ag_go(k, ag, b, 0, yup)
        ag_go(k, ag, b, 1, ydn)
        ag_go(k, ag, b, 1, yup)
        ag_go(k, ag, b, 0, ydn)

    def ag_end(k, ag, g):
        ag_arrived(k, ag, g * 4 + ym, 1)
        ag_arrived(k, ag, g * 4 + yp, 0)
        ag_arrived(k, ag, g * 4 + y2, 0)
        ag_arrived(k, ag, g * 4 + y2, 1)

    def group_rows(g):
        return pl.ds(al(g * GROUP, 16), GROUP)

    def project(lhs, weight, g, pb):
        def tile(j, carry):
            at = pl.ds(al(j * 256, 256), 256)
            pb[group_rows(g), at] = jnp.dot(
                lhs[group_rows(g), :], weight[:, at], preferred_element_type=F32
            ).astype(BF)
            return carry

        lax.fori_loop(0, D // 256, tile, 0)

    local_copies[4].wait()
    project(att, owv, o, pb1)
    rs_start(0, pb1, 0)
    project(att, owv, h, pb1)
    rs_start(0, pb1, 1)
    rs_middle(0, pb1, 0)
    rs_middle(0, pb1, 1)
    rs_cross(0, pb1)
    local_copies[5].wait()
    w_stage1()
    total = rs_total(0, pb1)
    mid = hidv[...].astype(F32) + normed(total, g_attn)
    resid[...] = mid
    ag1[rows_of(own_block), :] = normed(mid, g_pre).astype(BF)
    ag_start(0, ag1)
    ag_relay(0, ag1, h)
    ag_cross(0, ag1)
    w_stage2()
    ag_end(0, ag1, h)
    ag_relay(0, ag1, o)
    w_stage3()
    w_stage4()
    w_stage5()

    def ffn(g):
        def tile(j, carry):
            at = pl.ds(al(j * 128, 128), 128)
            both = jnp.concatenate([wbuf[0, :, at], wbuf[1, :, at]], axis=1)
            joint = jnp.dot(ag1[group_rows(g), :], both, preferred_element_type=F32)
            gate = joint[:, :128]
            up = joint[:, 128:]
            inner = 0.7978845608028654 * (gate + 0.044715 * (gate * gate * gate))
            act[group_rows(g), at] = (0.5 * gate * (1.0 + jnp.tanh(inner)) * up).astype(BF)
            return carry

        lax.fori_loop(0, UNITS // 128, tile, 0)

    ffn(h)
    ag_end(0, ag1, o)
    ffn(o)
    local_copies[6].wait()
    project(act, dwv, o, pb2)
    rs_start(1, pb2, 0)
    project(act, dwv, h, pb2)
    rs_start(1, pb2, 1)
    rs_middle(1, pb2, 0)
    rs_middle(1, pb2, 1)
    rs_cross(1, pb2)
    total = rs_total(1, pb2)
    last = resid[...] + normed(total, g_post)
    ag2[rows_of(own_block), :] = normed(last, g_next).astype(BF)
    ag_start(1, ag2)
    ag_relay(1, ag2, h)
    ag_cross(1, ag2)
    ag_end(1, ag2, h)
    ag_relay(1, ag2, o)
    local_copies[7].wait()

    def next_qkv(g):
        def tile(j, carry):
            at = pl.ds(al(j * 256, 256), 256)
            out[group_rows(g), at] = jnp.dot(
                ag2[group_rows(g), :], nwv[:, at], preferred_element_type=F32
            ).astype(BF)
            return carry

        lax.fori_loop(0, QKV // 256, tile, 0)

    next_qkv(h)
    ag_end(1, ag2, o)
    next_qkv(o)

    for sem, (cond, slot, dev) in enumerate(kv_sent):

        @pl.when(cond)
        def _(slot=slot, dev=dev, sem=sem):
            kv_send(slot, dev, sem).wait_send()

    for k in range(1, 8):
        a_send(k).wait_send()
    for sem, (slot, m, dev) in enumerate(w_sent):
        w_copy(slot, m, dev, sem).wait_send()
    for copy in rs_sent + ag_sent:
        copy.wait_send()


def local(hid, joined, lengths, ow, gu, dw, nw, g_attn, g_pre, g_post, g_next):
    hbm = pl.BlockSpec(memory_space=pl.ANY)
    vmem = pl.BlockSpec(memory_space=pltpu.VMEM)
    smem = pl.BlockSpec(memory_space=pltpu.SMEM)
    V = pltpu.VMEM
    DMA = pltpu.SemaphoreType.DMA
    scratch = [
        V((2, ROWS, HD), BF),
        V((16, ROWS, 2 * HD), BF),
        V(ow.shape, BF),
        V(dw.shape, BF),
        V(nw.shape, BF),
        V((BLK, D), BF),
        V(gu.shape, F32),
        V((8, 2, PIECE, UNITS), BF),
        V((8, 2, PIECE, UNITS), BF),
        V((2, D, UNITS), BF),
        V((2, ROWS, 1), F32),
        V((2, ROWS, 1), F32),
        V((2, ROWS, HD), F32),
        V((ROWS, 2 * HD), BF),
        V((ROWS, D), BF),
        V((ROWS, D), BF),
        V((2, 2, 2, BLK, HALF), BF),
        V((2, 2, 2, 2, BLK, HALF), BF),
        V((2, BLK, D), BF),
        V((2, BLK, D), BF),
        V((ROWS, D), BF),
        V((ROWS, D), BF),
        V((ROWS, UNITS), BF),
        V((BLK, D), F32),
        DMA((8,)),
        DMA((24,)),
        DMA((16,)),
        DMA((8,)),
        DMA((8,)),
        DMA((48,)),
        DMA((16, 2)),
        DMA((2, 2, 2)),
        DMA((2, 2, 2, 2)),
        DMA((2,)),
        DMA((32,)),
        DMA((40,)),
        DMA((2, 8, 2)),
    ]
    return pl.pallas_call(
        kernel,
        out_shape=jax.ShapeDtypeStruct((ROWS, QKV), BF),
        in_specs=[smem, hbm, hbm, hbm, hbm, hbm, hbm, vmem, vmem, vmem, vmem],
        out_specs=vmem,
        scratch_shapes=scratch,
        compiler_params=pltpu.CompilerParams(
            collective_id=0, has_side_effects=True, vmem_limit_bytes=67043328
        ),
    )(
        lengths, hid, joined, ow, gu, dw, nw,
        g_attn.reshape(1, D), g_pre.reshape(1, D), g_post.reshape(1, D), g_next.reshape(1, D),
    )


def solution(mesh):
    in_specs = (
        P("seq", None),
        P("seq", "tp"),
        P(),
        P("tp", None),
        P(None, ("seq", "tp"), None),
        P("tp", None),
        P(None, "tp"),
        P(),
        P(),
        P(),
        P(),
    )
    return jax.shard_map(
        local, mesh=mesh, in_specs=in_specs, out_specs=P("seq", "tp"), check_vma=False
    )
```

time: 498 us -> 182 us (0.37)
  waiting for transfers between devices: 317 us -> 0 us
  Pallas kernels: 0 us -> 171 us
  local copies, waits for them, and re-layouts: 71 us -> 10.5 us
  matrix products: 54.3 us -> 0 us
  blocking collectives: 21.5 us -> 0 us
  other arithmetic: 19.9 us -> 0 us
  between operations: 13.7 us -> 0.01 us
    all_gather x5 -> x0, waiting for transfers between devices: 219 us -> none  [the longest x1 70.7 us: local(): local_units = lax.all_gather(unit_rows, 'seq', axis=1, tiled=True)]
    pallas_call x0 -> x1, Pallas kernels: none -> 171 us  [local(): pl.pallas_call(kernel, out_shape=jax.ShapeDtypeStruct((ROWS, QKV), BF), i...]
    reduce_scatter x2 -> x0, waiting for transfers between devices: 96.9 us -> none  [scattered(): lax.psum_scatter(values.astype(jnp.bfloat16), 'tp', scatter_dimension=0,...]
    dot_general x6 -> x0, matrix products: 54.3 us -> none  [the longest x1 15.2 us: local(): jnp.dot(activated, down_weight, preferred_element_type=jnp.float32)]
    slice x4 -> x0, local copies, waits for them, and re-layouts: 29 us -> none  [the longest x1 26 us: local(): gate = jnp.dot(ffw_in, local_units[0], preferred_element_type=jnp.float32)]
    all_to_all x1 -> x0, blocking collectives: 21.5 us -> none  [local(): lax.all_to_all(server_low, 'tp', split_axis=2, concat_axis=1, tiled=True)]
    unnamed x21 -> x2, local copies, waits for them, and re-layouts: 25.8 us -> 5.24 us
    reduce_sum x6 -> x0, other arithmetic: 11.3 us -> none  [the longest x1 6.14 us: local(): norm_sum = jnp.sum(weights, axis=-1)]
  transfers between devices with their start and end apart: 7 -> 0, of which waited for: 7 -> 0; matrix products, arithmetic and copies ran while one was open for 17% -> 0% of each run, Pallas kernels for 0% -> 0%
where the time goes in v2:
time: 182 us; the launch traced here: 181 us
  Pallas kernels  171 us (94%)
  local copies, waits for them, and re-layouts  10.5 us (6%)
    pallas_call x1, Pallas kernels, local(): pl.pallas_call(kernel, out_shape=jax.ShapeDtypeStruct((ROWS, QKV), BF), i...  171 us
    unnamed x2, local copies, waits for them, and re-layouts  5.24 us

profile of v2, /device:TPU:1, one launch (start us, length us, event | category | flops | bytes accessed | tf_op | source)
XLA Modules:
  0.0 181.4 jit_solution(1384287722278617275)
XLA Ops:
  0.0 1.3 reshape.12.g_attn
  1.3 1.3 reshape.13.g_pre
  2.7 1.3 reshape.14.g_post
  4.0 1.3 reshape.15.g_next
  5.3 3.2 %copy.12.gu = f32[2,28,7168]{2,1,0:T(8,128)} copy(f32[2,28,7168]{2,0,1:T(2,128)} %param.15) | data formatting | bytes 3211264 | tf_op args[4]
  8.5 170.9 %shard_map.109 = bf16[384,1024]{1,0:T(8,128)(2,1)} custom-call(s32[4]{0:T(128)} %lens.1, bf16[384,3584]{1,0:T(8,128)(2,1)} %hid.1, bf16[384,1024]{1,0:T(8,128)(2,1)} %joined.1, bf16[512,3584]{1,0:T(8,128)(2,1)} %ow.1, f32[2,28,7168]{2,1,0:T(8,128)} %copy.12.gu, bf16[896,3584]{1,0:T(8,128)(2,1)} %dw.1, bf16[3584,1024]{1,0:T(8,128)(2,1)} %nw.1, ...), custom_call_target="tpu_custom_call" | custom-call | tf_op jit(solution)/shard_map/pallas_call | solution.py:594
  179.4 2.1 %copy.14 = bf16[384,1024]{1,0:T(8,128)(2,1)} copy(bf16[384,1024]{1,0:T(8,128)(2,1)} %shard_map.109) | data formatting | bytes 1572864

commit v3 on v2

--- a/solution.py
+++ b/solution.py
@@ -64,7 +64,7 @@
 
     own_block = h * 4 + y
     loads = [
-        (joined.at[:, pl.ds(512, 512)], kvbuf.at[s]),
+        (joined.at[:, pl.ds(512, 256)], kvbuf.at[s, 0]),
         (joined.at[:, pl.ds(0, 256)], qbuf.at[0]),
         (joined.at[:, pl.ds(256, 256)], qbuf.at[1]),
         (gu, guv),
@@ -72,6 +72,7 @@
         (hid.at[pl.ds(al(own_block * BLK, 16), BLK), :], hidv),
         (dw, dwv),
         (nw, nwv),
+        (joined.at[:, pl.ds(768, 256)], kvbuf.at[s, 1]),
     ]
     local_copies = [
         pltpu.make_async_copy(src, dst, lsem.at[i]) for i, (src, dst) in enumerate(loads)
@@ -91,32 +92,28 @@
 
     pl.semaphore_wait(barrier, 11)
 
-    def kv_send(slot, dev, sem):
-        return rcopy(kvbuf.at[slot], kvbuf.at[slot], kv_s.at[sem], kv_r.at[slot], dev)
-
-    def kv_arrived(slot):
-        kv_send(slot, sib, 0).wait_recv()
+    def kv_send(slot, part, dev, sem):
+        ref = kvbuf.at[slot, part]
+        return rcopy(ref, ref, kv_s.at[sem], kv_r.at[slot, part], dev)
+
+    def kv_arrived(slot, part):
+        kv_send(slot, part, sib, 0).wait_recv()
 
     kv_sent = []
-
-    def kv_go(cond, slot, dev):
-        sem = len(kv_sent)
-        kv_sent.append((cond, slot, dev))
-
-        @pl.when(cond)
-        def _():
-            kv_send(slot, dev, sem).start()
-
-    local_copies[0].wait()
-    always = s >= 0
-    kv_go(z < 3, s, zup)
-    kv_go(x == 0, s, xnb)
-    kv_go(z == 0, s, zdn)
-    kv_go(c == 0, s, sib)
+    for part in range(2):
+        local_copies[(0, 8)[part]].wait()
+        for ok, dev in ((z < 3, zup), (x == 0, xnb), (z == 0, zdn), (c == 0, sib)):
+            sem = len(kv_sent)
+            kv_sent.append((ok, s, part, dev))
+
+            @pl.when(ok)
+            def _(part=part, dev=dev, sem=sem):
+                kv_send(s, part, dev, sem).start()
 
     local_copies[3].wait()
     for k in range(8):
-        gub[k] = guv[:, :, k * UNITS : (k + 1) * UNITS].astype(BF)
+        for m in range(2):
+            gub[k, m] = guv[:, m, k * UNITS : (k + 1) * UNITS].astype(BF)
 
     def a_send(k):
         peer = (t + k) % 8
@@ -148,7 +145,7 @@
         def head(r, carry):
             scores = lax.dot_general(
                 qbuf[r],
-                kvbuf[slot, :, 0:HD],
+                kvbuf[slot, 0],
                 (((1,), (1,)), ((), ())),
                 preferred_element_type=F32,
             ) * (HD ** -0.5)
@@ -160,7 +157,7 @@
             lbuf[r] = lbuf[r] * fade + jnp.sum(weights, axis=-1, keepdims=True)
             mbuf[r] = peak
             acc[r] = acc[r] * fade + jnp.dot(
-                weights.astype(BF), kvbuf[slot, :, HD : 2 * HD], preferred_element_type=F32
+                weights.astype(BF), kvbuf[slot, 1], preferred_element_type=F32
             )
             return carry
 
@@ -202,45 +199,55 @@
             rows = jnp.concatenate([abuf[k, m].astype(F32) for k in range(8)], axis=0)
             wbuf[m, pl.ds(al(s * CHUNK, 16), CHUNK), :] = rows.astype(BF)
 
+    def w_first():
+        for m in range(2):
+            w_go(s, m, xnb)
+        for m in range(2):
+            w_go(s, m, sib)
+
+    def w_second():
+        w_go(s, 0, zup)
+        w_go(s, 1, zdn)
+        w_go(s, 1, zup)
+        w_go(s, 0, zdn)
+
     def comm_of(entries):
         plan = []
-        for cond, slot, forward, relays in entries:
-            sends = [(cond if forward is None else cond & forward, sib)] + relays
+        for part, (cond, slot, forward, relays) in entries:
+            sends = relays + [(cond if forward is None else cond & forward, sib)]
             numbered = []
             for ok, dev in sends:
                 numbered.append((ok, dev, len(kv_sent)))
-                kv_sent.append((ok, slot, dev))
-            plan.append((cond, slot, numbered))
+                kv_sent.append((ok, slot, part, dev))
+            plan.append((cond, slot, part, numbered))
 
         def run():
-            for cond, slot, numbered in plan:
+            for cond, slot, part, numbered in plan:
 
                 @pl.when(cond)
-                def _(slot=slot):
-                    kv_arrived(slot)
-
-                for ok, dev, sem in numbered[1:] + numbered[:1]:
+                def _(slot=slot, part=part):
+                    kv_arrived(slot, part)
+
+                for ok, dev, sem in numbered:
 
                     @pl.when(ok)
-                    def _(slot=slot, dev=dev, sem=sem):
-                        kv_send(slot, dev, sem).start()
+                    def _(slot=slot, part=part, dev=dev, sem=sem):
+                        kv_send(slot, part, dev, sem).start()
 
         return run
 
     middle = (z == 1) | (z == 2)
-    comm_a = comm_of([
-        (up_ok(-1), up_slot(-1, c), None, [(middle, zup)]),
-        (down_ok(0), down_slot(0, c), c == 1, [((x == 1) & (z >= 1), zdn), ((x == 1) & (z == 3), zup)]),
-    ])
-    comm_b = comm_of([
-        (down_ok(1), down_slot(1, c), None, [((x == 1) & middle, zdn)]),
-        (up_ok(-3), up_slot(-3, c), None, []),
-        (down_ok(3), down_slot(3, c), None, []),
-    ])
-    comm_c = comm_of([
-        (up_ok(-2), up_slot(-2, c), None, []),
-        (down_ok(2), down_slot(2, c), None, []),
-    ])
+    up1 = (up_ok(-1), up_slot(-1, c), None, [(middle, zup)])
+    over = (down_ok(0), down_slot(0, c), c == 1, [((x == 1) & (z >= 1), zdn), ((x == 1) & (z == 3), zup)])
+    down1 = (down_ok(1), down_slot(1, c), None, [((x == 1) & middle, zdn)])
+    up3 = (up_ok(-3), up_slot(-3, c), None, [])
+    down3 = (down_ok(3), down_slot(3, c), None, [])
+    up2 = (up_ok(-2), up_slot(-2, c), None, [])
+    down2 = (down_ok(2), down_slot(2, c), None, [])
+    comm_a = comm_of([(0, over), (0, up1), (1, over), (1, up1)])
+    comm_b0 = comm_of([(0, down1)])
+    comm_b1 = comm_of([(1, down1), (0, up3), (1, up3), (0, down3), (1, down3)])
+    comm_c = comm_of([(0, up2), (0, down2), (1, up2), (1, down2)])
 
     offsets = {2: -1, 3: 0, 4: -1, 5: 0, 6: 1, 7: -3, 8: 3, 9: 1, 10: -3, 11: 3, 12: -2, 13: 2, 14: -2, 15: 2}
 
@@ -249,9 +256,16 @@
         def _():
             comm_a()
 
+        @pl.when(i == 4)
+        def _():
+            comm_b0()
+            repack()
+            w_first()
+
         @pl.when(i == 6)
         def _():
-            comm_b()
+            comm_b1()
+            w_second()
 
         @pl.when(i == 12)
         def _():
@@ -271,7 +285,8 @@
 
         @pl.when(ok & from_sib)
         def _():
-            kv_arrived(slot)
+            kv_arrived(slot, 0)
+            kv_arrived(slot, 1)
 
         @pl.when(ok)
         def _():
@@ -281,18 +296,8 @@
 
     lax.fori_loop(0, 16, step, 0)
 
-    repack()
     for r in range(2):
         att[:, r * HD : (r + 1) * HD] = (acc[r] / lbuf[r, :, 0:1]).astype(BF)
-
-    for m in range(2):
-        w_go(s, m, xnb)
-    w_go(s, 0, zup)
-    w_go(s, 1, zdn)
-    w_go(s, 1, zup)
-    w_go(s, 0, zdn)
-    for m in range(2):
-        w_go(s, m, sib)
 
     s_x = (1 - x) * 8 + z * 2 + c
     s_zm = x * 8 + zm * 2 + c
@@ -401,7 +406,7 @@
 
     def normed(values, gain):
         meansq = jnp.mean(values * values, axis=-1, keepdims=True)
-        return values * lax.rsqrt(meansq + 1e-06) * gain[...]
+        return values * lax.rsqrt(meansq + 1e-06) * gain[...].reshape(1, D)
 
     ag_sent = []
 
@@ -464,22 +469,22 @@
     project(att, owv, o, pb1)
     rs_start(0, pb1, 0)
     project(att, owv, h, pb1)
+    rs_middle(0, pb1, 0)
     rs_start(0, pb1, 1)
-    rs_middle(0, pb1, 0)
+    rs_cross(0, pb1)
     rs_middle(0, pb1, 1)
-    rs_cross(0, pb1)
+    w_stage1()
     local_copies[5].wait()
-    w_stage1()
     total = rs_total(0, pb1)
     mid = hidv[...].astype(F32) + normed(total, g_attn)
     resid[...] = mid
     ag1[rows_of(own_block), :] = normed(mid, g_pre).astype(BF)
     ag_start(0, ag1)
+    w_stage2()
     ag_relay(0, ag1, h)
     ag_cross(0, ag1)
-    w_stage2()
+    ag_relay(0, ag1, o)
     ag_end(0, ag1, h)
-    ag_relay(0, ag1, o)
     w_stage3()
     w_stage4()
     w_stage5()
@@ -504,10 +509,10 @@
     project(act, dwv, o, pb2)
     rs_start(1, pb2, 0)
     project(act, dwv, h, pb2)
+    rs_middle(1, pb2, 0)
     rs_start(1, pb2, 1)
-    rs_middle(1, pb2, 0)
+    rs_cross(1, pb2)
     rs_middle(1, pb2, 1)
-    rs_cross(1, pb2)
     total = rs_total(1, pb2)
     last = resid[...] + normed(total, g_post)
     ag2[rows_of(own_block), :] = normed(last, g_next).astype(BF)
@@ -532,11 +537,11 @@
     ag_end(1, ag2, o)
     next_qkv(o)
 
-    for sem, (cond, slot, dev) in enumerate(kv_sent):
+    for sem, (cond, slot, part, dev) in enumerate(kv_sent):
 
         @pl.when(cond)
-        def _(slot=slot, dev=dev, sem=sem):
-            kv_send(slot, dev, sem).wait_send()
+        def _(slot=slot, part=part, dev=dev, sem=sem):
+            kv_send(slot, part, dev, sem).wait_send()
 
     for k in range(1, 8):
         a_send(k).wait_send()
@@ -554,12 +559,12 @@
     DMA = pltpu.SemaphoreType.DMA
     scratch = [
         V((2, ROWS, HD), BF),
-        V((16, ROWS, 2 * HD), BF),
+        V((16, 2, ROWS, HD), BF),
         V(ow.shape, BF),
         V(dw.shape, BF),
         V(nw.shape, BF),
         V((BLK, D), BF),
-        V(gu.shape, F32),
+        V((PIECE, 2, gu.shape[2]), F32),
         V((8, 2, PIECE, UNITS), BF),
         V((8, 2, PIECE, UNITS), BF),
         V((2, D, UNITS), BF),
@@ -577,9 +582,9 @@
         V((ROWS, D), BF),
         V((ROWS, UNITS), BF),
         V((BLK, D), F32),
-        DMA((8,)),
-        DMA((24,)),
-        DMA((16,)),
+        DMA((9,)),
+        DMA((36,)),
+        DMA((16, 2)),
         DMA((8,)),
         DMA((8,)),
         DMA((48,)),
@@ -601,8 +606,8 @@
             collective_id=0, has_side_effects=True, vmem_limit_bytes=67043328
         ),
     )(
-        lengths, hid, joined, ow, gu, dw, nw,
-        g_attn.reshape(1, D), g_pre.reshape(1, D), g_post.reshape(1, D), g_next.reshape(1, D),
+        lengths, hid, joined, ow, gu.transpose(1, 0, 2), dw, nw,
+        g_attn, g_pre, g_post, g_next,
     )
 
 

time: 182 us -> 163 us (0.90)
  Pallas kernels: 171 us -> 161 us
  local copies, waits for them, and re-layouts: 10.5 us -> 2.06 us
    pallas_call x1, Pallas kernels: 171 us -> 161 us  [local(): pl.pallas_call(kernel, out_shape=jax.ShapeDtypeStruct((ROWS, QKV), BF), i...]
    reshape x4 -> x0, local copies, waits for them, and re-layouts: 5.3 us -> none  [the longest x1 1.33 us: local(): g_next.reshape(1, D)]
    unnamed x2 -> x1, local copies, waits for them, and re-layouts: 5.24 us -> 2.06 us
where the time goes in v3:
time: 163 us
  Pallas kernels  161 us (99%)
  local copies, waits for them, and re-layouts  2.06 us (1%)
    pallas_call x1, Pallas kernels, local(): pl.pallas_call(kernel, out_shape=jax.ShapeDtypeStruct((ROWS, QKV), BF), i...  161 us

profile of v3, /device:TPU:1, one launch (start us, length us, event | category | flops | bytes accessed | tf_op | source)
XLA Modules:
  0.0 163.1 jit_solution(16712145654852130319)
XLA Ops:
  0.0 161.0 %shard_map.109 = bf16[384,1024]{1,0:T(8,128)(2,1)} custom-call(s32[4]{0:T(128)} %lens.1, bf16[384,3584]{1,0:T(8,128)(2,1)} %hid.1, bf16[384,1024]{1,0:T(8,128)(2,1)} %joined.1, bf16[512,3584]{1,0:T(8,128)(2,1)} %ow.1, f32[28,2,7168]{2,1,0:T(2,128)} %bitcast.1, bf16[896,3584]{1,0:T(8,128)(2,1)} %dw.1, bf16[3584,1024]{1,0:T(8,128)(2,1)} %nw.1, f32[3584]{0:T(1024)} %g_attn.1, ...), custom_call_target="tpu_custom_call" | custom-call | tf_op jit(solution)/shard_map/pallas_call | solution.py:599
  161.0 2.1 %copy.13 = bf16[384,1024]{1,0:T(8,128)(2,1)} copy(bf16[384,1024]{1,0:T(8,128)(2,1)} %shard_map.109) | data formatting | bytes 1572864

commit v4 on v3

--- a/solution.py
+++ b/solution.py
@@ -9,7 +9,8 @@
 BF = jnp.bfloat16
 F32 = jnp.float32
 D = 3584
-HALF = D // 2
+PART_A = 1536
+PART_B = D - PART_A
 ROWS = 384
 HD = 256
 UNITS = 896
@@ -29,8 +30,8 @@
     lens, hid, joined, ow, gu, dw, nw, g_attn, g_pre, g_post, g_next,
     out,
     qbuf, kvbuf, owv, dwv, nwv, hidv, guv, gub, abuf, wbuf,
-    mbuf, lbuf, acc, att, pb1, pb2, r1, r2, rx, sx, ag1, ag2, act, resid,
-    lsem, kv_s, kv_r, a_s, a_r, w_s, w_r, r1_r, r2_r, rx_r, rs_s, ag_s, ag_r,
+    mbuf, lbuf, acc, att, pb1, pb2, r1b, r2b, r1a, r2a, rxa, rx, sx, ag1, ag2, act, resid,
+    lsem, kv_s, kv_r, a_s, a_r, w_s, w_r, r1_r, r2_r, rxa_r, rx_r, rs_s, ag_s, ag_r,
 ):
     s = lax.axis_index("seq")
     t = lax.axis_index("tp")
@@ -307,41 +308,44 @@
     s_xzp = (1 - x) * 8 + zp * 2 + c
     s_xz2 = (1 - x) * 8 + (z + 2) % 4 * 2 + c
 
-    def w_stage1():
-        w_arrived(s_zm, 0)
-        w_go(s_zm, 0, zup)
-        w_arrived(s_zp, 1)
-        w_go(s_zp, 1, zdn)
+    def w_over():
         for m in range(2):
             w_arrived(s_x, m)
         w_go(s_x, 0, zup)
         w_go(s_x, 1, zdn)
         w_go(s_x, 1, zup)
         w_go(s_x, 0, zdn)
+        for m in range(2):
+            w_go(s_x, m, sib)
+
+    def w_relay():
+        w_arrived(s_zm, 0)
+        w_go(s_zm, 0, zup)
+        w_arrived(s_zp, 1)
+        w_go(s_zp, 1, zdn)
         w_arrived(s_zm, 1)
         w_arrived(s_zp, 0)
-        for slot in (s_x, s_zm, s_zp):
+        for slot in (s_zm, s_zp):
             for m in range(2):
                 w_go(slot, m, sib)
 
-    def w_stage2():
+    def w_relay_over():
+        w_arrived(s_xzm, 0)
+        w_go(s_xzm, 0, zup)
+        w_arrived(s_xzp, 1)
+        w_go(s_xzp, 1, zdn)
+        w_arrived(s_xzm, 1)
+        w_arrived(s_xzp, 0)
         for m in range(2):
             w_arrived(s_z2, m)
-            w_go(s_z2, m, xnb)
-            w_go(s_z2, m, sib)
-
-    def w_stage3():
-        for slot in (s_xzm, s_xzp):
+        for slot in (s_xzm, s_xzp, s_z2):
             for m in range(2):
-                w_arrived(slot, m)
                 w_go(slot, m, sib)
 
-    def w_stage4():
+    def w_end():
         for m in range(2):
             w_arrived(s_xz2, m)
             w_go(s_xz2, m, sib)
-
-    def w_stage5():
         for xx in range(2):
             for zz in range(4):
                 for m in range(2):
@@ -357,52 +361,94 @@
     def rows_of(block):
         return pl.ds(al(block * BLK, 16), BLK)
 
-    cols = (pl.ds(0, HALF), pl.ds(HALF, HALF))
-    phase_h = (o, h)
-
-    def rs_start(k, pb, p):
-        g = phase_h[p]
+    cols = (
+        (pl.ds(0, PART_A // 2), pl.ds(PART_A // 2, PART_A // 2)),
+        (pl.ds(PART_A, PART_B // 2), pl.ds(PART_A + PART_B // 2, PART_B // 2)),
+    )
+    first = pl.ds(0, PART_A)
+    lanes = ((1, o), (1, h), (0, h))
+
+    def r1_at(k, lane, way):
+        return r1b.at[k, lane, way] if lane < 2 else r1a.at[k, way]
+
+    def r2_at(k, lane, way, half):
+        return r2b.at[k, lane, way, half] if lane < 2 else r2a.at[k, way, half]
+
+    def arrived(ref, recv):
+        rcopy(ref, ref, rs_s.at[0], recv, xhi).wait_recv()
+
+    def rs_far(k, pb, lane):
+        part, g = lanes[lane]
         far = rows_of(g * 4 + y2)
-        send(pb.at[far, cols[0]], r1.at[k, p, 0], r1_r.at[k, p, 0], yup)
-        send(pb.at[far, cols[1]], r1.at[k, p, 1], r1_r.at[k, p, 1], ydn)
-        send(pb.at[rows_of(g * 4 + yp), cols[1]], r2.at[k, p, 0, 1], r2_r.at[k, p, 0, 1], yup)
-        send(pb.at[rows_of(g * 4 + ym), cols[0]], r2.at[k, p, 1, 0], r2_r.at[k, p, 1, 0], ydn)
-
-    def rs_middle(k, pb, p):
-        g = phase_h[p]
+        send(pb.at[far, cols[part][0]], r1_at(k, lane, 0), r1_r.at[k, lane, 0], yup)
+        send(pb.at[far, cols[part][1]], r1_at(k, lane, 1), r1_r.at[k, lane, 1], ydn)
+
+    def rs_near(k, pb, lane):
+        part, g = lanes[lane]
+        send(pb.at[rows_of(g * 4 + yp), cols[part][1]], r2_at(k, lane, 0, 1), r2_r.at[k, lane, 0, 1], yup)
+        send(pb.at[rows_of(g * 4 + ym), cols[part][0]], r2_at(k, lane, 1, 0), r2_r.at[k, lane, 1, 0], ydn)
+
+    def rs_middle(k, pb, lane):
+        part, g = lanes[lane]
         for way, (yy, dev) in enumerate(((yp, yup), (ym, ydn))):
             near = rows_of(g * 4 + yy)
-            rcopy(r1.at[k, p, way], r1.at[k, p, way], rs_s.at[0], r1_r.at[k, p, way], dev).wait_recv()
-            pb[near, cols[way]] = (
-                pb[near, cols[way]].astype(F32) + r1[k, p, way].astype(F32)
+            ref = r1_at(k, lane, way)
+            arrived(ref, r1_r.at[k, lane, way])
+            pb[near, cols[part][way]] = (
+                pb[near, cols[part][way]].astype(F32) + ref[...].astype(F32)
             ).astype(BF)
-            send(pb.at[near, cols[way]], r2.at[k, p, way, way], r2_r.at[k, p, way, way], dev)
-
-    def rs_end(k, pb, p):
-        g = phase_h[p]
+            send(pb.at[near, cols[part][way]], r2_at(k, lane, way, way), r2_r.at[k, lane, way, way], dev)
+
+    def rs_end(k, pb, lane):
+        part, g = lanes[lane]
         for way in range(2):
             for half in range(2):
-                ref = r2.at[k, p, way, half]
-                rcopy(ref, ref, rs_s.at[0], r2_r.at[k, p, way, half], yup).wait_recv()
+                arrived(r2_at(k, lane, way, half), r2_r.at[k, lane, way, half])
         mine = rows_of(g * 4 + y)
         return jnp.concatenate(
             [
-                pb[mine, cols[half]].astype(F32)
-                + r2[k, p, 0, half].astype(F32)
-                + r2[k, p, 1, half].astype(F32)
+                pb[mine, cols[part][half]].astype(F32)
+                + r2_at(k, lane, 0, half)[...].astype(F32)
+                + r2_at(k, lane, 1, half)[...].astype(F32)
                 for half in range(2)
             ],
             axis=1,
         )
 
-    def rs_cross(k, pb):
+    def rs_over(k, pb):
+        for yy in (y2, yp, ym, y):
+            send(pb.at[rows_of(o * 4 + yy), first], rxa.at[k, yy], rxa_r.at[k, yy], xhi)
+
+    def rs_add(k, pb, yy):
+        arrived(rxa.at[k, yy], rxa_r.at[k, yy])
+        at = rows_of(h * 4 + yy)
+        pb[at, first] = (pb[at, first].astype(F32) + rxa[k, yy].astype(F32)).astype(BF)
+
+    def tp_sum(k, lhs, weight, pb, pump0, pump1):
+        project(lhs, weight, o, pb)
+        rs_over(k, pb)
+        rs_far(k, pb, 0)
+        rs_near(k, pb, 0)
+        project(lhs, weight, h, pb)
+        rs_middle(k, pb, 0)
+        pump0()
+        rs_add(k, pb, y2)
+        rs_far(k, pb, 2)
+        rs_far(k, pb, 1)
+        rs_near(k, pb, 1)
         sx[k] = rs_end(k, pb, 0).astype(BF)
         send(sx.at[k], rx.at[k], rx_r.at[k], xhi)
-
-    def rs_total(k, pb):
-        total = rs_end(k, pb, 1)
-        rcopy(rx.at[k], rx.at[k], rs_s.at[0], rx_r.at[k], xhi).wait_recv()
-        return total + rx[k].astype(F32)
+        rs_middle(k, pb, 1)
+        rs_add(k, pb, yp)
+        rs_add(k, pb, ym)
+        rs_near(k, pb, 2)
+        rs_middle(k, pb, 2)
+        pump1()
+        part_b = rs_end(k, pb, 1)
+        arrived(rxa.at[k, y], rxa_r.at[k, y])
+        part_a = rs_end(k, pb, 2) + rxa[k, y].astype(F32)
+        arrived(rx.at[k], rx_r.at[k])
+        return jnp.concatenate([part_a, part_b + rx[k].astype(F32)], axis=1)
 
     def normed(values, gain):
         meansq = jnp.mean(values * values, axis=-1, keepdims=True)
@@ -410,47 +456,70 @@
 
     ag_sent = []
 
-    def ag_copy(k, ag, block, half, dev, sem):
-        ref = ag.at[rows_of(block), cols[half]]
-        return rcopy(ref, ref, ag_s.at[sem], ag_r.at[k, block, half], dev)
-
-    def ag_go(k, ag, block, half, dev):
-        copy = ag_copy(k, ag, block, half, dev, len(ag_sent))
+    def ag_copy(k, ag, block, part, half, dev, sem):
+        ref = ag.at[rows_of(block), cols[part][half]]
+        return rcopy(ref, ref, ag_s.at[sem], ag_r.at[k, block, part * 2 + half], dev)
+
+    def ag_go(k, ag, block, part, half, dev):
+        copy = ag_copy(k, ag, block, part, half, dev, len(ag_sent))
         copy.start()
         ag_sent.append(copy)
 
-    def ag_arrived(k, ag, block, half):
-        ag_copy(k, ag, block, half, xhi, 0).wait_recv()
-
-    def ag_start(k, ag):
-        b = h * 4 + y
-        ag_go(k, ag, b, 0, xhi)
-        ag_go(k, ag, b, 1, xhi)
-        ag_go(k, ag, b, 0, yup)
-        ag_go(k, ag, b, 1, ydn)
-        ag_go(k, ag, b, 1, yup)
-        ag_go(k, ag, b, 0, ydn)
-
-    def ag_relay(k, ag, g):
-        ag_arrived(k, ag, g * 4 + ym, 0)
-        ag_go(k, ag, g * 4 + ym, 0, yup)
-        ag_arrived(k, ag, g * 4 + yp, 1)
-        ag_go(k, ag, g * 4 + yp, 1, ydn)
-
-    def ag_cross(k, ag):
-        b = o * 4 + y
+    def ag_arrived(k, ag, block, part, half):
+        ag_copy(k, ag, block, part, half, xhi, 0).wait_recv()
+
+    def ag_both(k, ag, block, part):
+        ag_go(k, ag, block, part, 0, yup)
+        ag_go(k, ag, block, part, 1, ydn)
+        ag_go(k, ag, block, part, 1, yup)
+        ag_go(k, ag, block, part, 0, ydn)
+
+    def ag_relay(k, ag, g, part):
+        ag_arrived(k, ag, g * 4 + ym, part, 0)
+        ag_go(k, ag, g * 4 + ym, part, 0, yup)
+        ag_arrived(k, ag, g * 4 + yp, part, 1)
+        ag_go(k, ag, g * 4 + yp, part, 1, ydn)
+
+    def ag_rest(k, ag, g, part):
+        ag_arrived(k, ag, g * 4 + ym, part, 1)
+        ag_arrived(k, ag, g * 4 + yp, part, 0)
+
+    def ag_far(k, ag, g, part):
+        ag_arrived(k, ag, g * 4 + y2, part, 0)
+        ag_arrived(k, ag, g * 4 + y2, part, 1)
+
+    def tp_gather(k, ag, pump0, pump1):
+        own = h * 4 + y
         for half in range(2):
-            ag_arrived(k, ag, b, half)
-        ag_go(k, ag, b, 0, yup)
-        ag_go(k, ag, b, 1, ydn)
-        ag_go(k, ag, b, 1, yup)
-        ag_go(k, ag, b, 0, ydn)
-
-    def ag_end(k, ag, g):
-        ag_arrived(k, ag, g * 4 + ym, 1)
-        ag_arrived(k, ag, g * 4 + yp, 0)
-        ag_arrived(k, ag, g * 4 + y2, 0)
-        ag_arrived(k, ag, g * 4 + y2, 1)
+            ag_go(k, ag, own, 1, half, xhi)
+        ag_both(k, ag, own, 0)
+        for half in range(2):
+            ag_go(k, ag, own, 0, half, xhi)
+        ag_both(k, ag, own, 1)
+        ag_relay(k, ag, h, 0)
+        ag_rest(k, ag, h, 0)
+        for yy in (ym, yp):
+            for half in range(2):
+                ag_go(k, ag, h * 4 + yy, 0, half, xhi)
+        pump0()
+        for half in range(2):
+            ag_arrived(k, ag, o * 4 + y, 1, half)
+        ag_relay(k, ag, h, 1)
+        ag_both(k, ag, o * 4 + y, 1)
+        ag_far(k, ag, h, 0)
+        for half in range(2):
+            ag_go(k, ag, h * 4 + y2, 0, half, xhi)
+        pump1()
+        ag_relay(k, ag, o, 1)
+        ag_rest(k, ag, h, 1)
+        ag_far(k, ag, h, 1)
+
+    def tp_gathered(k, ag):
+        ag_rest(k, ag, o, 1)
+        ag_far(k, ag, o, 1)
+        for yy in range(4):
+            for half in range(2):
+                ag_arrived(k, ag, o * 4 + yy, 0, half)
 
     def group_rows(g):
         return pl.ds(al(g * GROUP, 16), GROUP)
@@ -465,29 +534,18 @@
 
         lax.fori_loop(0, D // 256, tile, 0)
 
+    def nothing():
+        pass
+
     local_copies[4].wait()
-    project(att, owv, o, pb1)
-    rs_start(0, pb1, 0)
-    project(att, owv, h, pb1)
-    rs_middle(0, pb1, 0)
-    rs_start(0, pb1, 1)
-    rs_cross(0, pb1)
-    rs_middle(0, pb1, 1)
-    w_stage1()
+    w_over()
+    total = tp_sum(0, att, owv, pb1, nothing, w_relay)
     local_copies[5].wait()
-    total = rs_total(0, pb1)
     mid = hidv[...].astype(F32) + normed(total, g_attn)
     resid[...] = mid
     ag1[rows_of(own_block), :] = normed(mid, g_pre).astype(BF)
-    ag_start(0, ag1)
-    w_stage2()
-    ag_relay(0, ag1, h)
-    ag_cross(0, ag1)
-    ag_relay(0, ag1, o)
-    ag_end(0, ag1, h)
-    w_stage3()
-    w_stage4()
-    w_stage5()
+    tp_gather(0, ag1, nothing, w_relay_over)
+    w_end()
 
     def ffn(g):
         def tile(j, carry):
@@ -503,24 +561,13 @@
         lax.fori_loop(0, UNITS // 128, tile, 0)
 
     ffn(h)
-    ag_end(0, ag1, o)
+    tp_gathered(0, ag1)
     ffn(o)
     local_copies[6].wait()
-    project(act, dwv, o, pb2)
-    rs_start(1, pb2, 0)
-    project(act, dwv, h, pb2)
-    rs_middle(1, pb2, 0)
-    rs_start(1, pb2, 1)
-    rs_cross(1, pb2)
-    rs_middle(1, pb2, 1)
-    total = rs_total(1, pb2)
+    total = tp_sum(1, act, dwv, pb2, nothing, nothing)
     last = resid[...] + normed(total, g_post)
     ag2[rows_of(own_block), :] = normed(last, g_next).astype(BF)
-    ag_start(1, ag2)
-    ag_relay(1, ag2, h)
-    ag_cross(1, ag2)
-    ag_end(1, ag2, h)
-    ag_relay(1, ag2, o)
+    tp_gather(1, ag2, nothing, nothing)
     local_copies[7].wait()
 
     def next_qkv(g):
@@ -534,7 +581,7 @@
         lax.fori_loop(0, QKV // 256, tile, 0)
 
     next_qkv(h)
-    ag_end(1, ag2, o)
+    tp_gathered(1, ag2)
     next_qkv(o)
 
     for sem, (cond, slot, part, dev) in enumerate(kv_sent):
@@ -574,10 +621,13 @@
         V((ROWS, 2 * HD), BF),
         V((ROWS, D), BF),
         V((ROWS, D), BF),
-        V((2, 2, 2, BLK, HALF), BF),
-        V((2, 2, 2, 2, BLK, HALF), BF),
-        V((2, BLK, D), BF),
-        V((2, BLK, D), BF),
+        V((2, 2, 2, BLK, PART_B // 2), BF),
+        V((2, 2, 2, 2, BLK, PART_B // 2), BF),
+        V((2, 2, BLK, PART_A // 2), BF),
+        V((2, 2, 2, BLK, PART_A // 2), BF),
+        V((2, 4, BLK, PART_A), BF),
+        V((2, BLK, PART_B), BF),
+        V((2, BLK, PART_B), BF),
         V((ROWS, D), BF),
         V((ROWS, D), BF),
         V((ROWS, UNITS), BF),
@@ -589,12 +639,13 @@
         DMA((8,)),
         DMA((48,)),
         DMA((16, 2)),
-        DMA((2, 2, 2)),
-        DMA((2, 2, 2, 2)),
+        DMA((2, 3, 2)),
+        DMA((2, 3, 2, 2)),
+        DMA((2, 4)),
         DMA((2,)),
-        DMA((32,)),
-        DMA((40,)),
-        DMA((2, 8, 2)),
+        DMA((48,)),
+        DMA((64,)),
+        DMA((2, 8, 4)),
     ]
     return pl.pallas_call(
         kernel,

time: 163 us -> 150 us (0.920)
  Pallas kernels: 161 us -> 146 us
    pallas_call x1, Pallas kernels: 161 us -> 146 us  [local(): pl.pallas_call(kernel, out_shape=jax.ShapeDtypeStruct((ROWS, QKV), BF), i...]
where the time goes in v4:
time: 150 us; the launch traced here: 149 us
  Pallas kernels  146 us (97%)
  local copies, waits for them, and re-layouts  2.06 us (1%)
    pallas_call x1, Pallas kernels, local(): pl.pallas_call(kernel, out_shape=jax.ShapeDtypeStruct((ROWS, QKV), BF), i...  146 us

profile of v4, /device:TPU:1, one launch (start us, length us, event | category | flops | bytes accessed | tf_op | source)
XLA Modules:
  0.0 148.5 jit_solution(7229512830707625517)
XLA Ops:
  0.0 146.4 %shard_map.109 = bf16[384,1024]{1,0:T(8,128)(2,1)} custom-call(s32[4]{0:T(128)} %lens.1, bf16[384,3584]{1,0:T(8,128)(2,1)} %hid.1, bf16[384,1024]{1,0:T(8,128)(2,1)} %joined.1, bf16[512,3584]{1,0:T(8,128)(2,1)} %ow.1, f32[28,2,7168]{2,1,0:T(2,128)} %bitcast.1, bf16[896,3584]{1,0:T(8,128)(2,1)} %dw.1, bf16[3584,1024]{1,0:T(8,128)(2,1)} %nw.1, f32[3584]{0:T(1024)} %g_attn.1, ...), custom_call_target="tpu_custom_call" | custom-call | tf_op jit(solution)/shard_map/pallas_call | solution.py:650
  146.4 2.1 %copy.13 = bf16[384,1024]{1,0:T(8,128)(2,1)} copy(bf16[384,1024]{1,0:T(8,128)(2,1)} %shard_map.109) | data formatting | bytes 1572864

commit v5 on v4

--- a/solution.py
+++ b/solution.py
@@ -30,7 +30,7 @@
     lens, hid, joined, ow, gu, dw, nw, g_attn, g_pre, g_post, g_next,
     out,
     qbuf, kvbuf, owv, dwv, nwv, hidv, guv, gub, abuf, wbuf,
-    mbuf, lbuf, acc, att, pb1, pb2, r1b, r2b, r1a, r2a, rxa, rx, sx, ag1, ag2, act, resid,
+    lowbuf, mbuf, lbuf, acc, att, pb1, pb2, r1b, r2b, r1a, r2a, rxa, rx, sx, ag1, ag2, act, resid,
     lsem, kv_s, kv_r, a_s, a_r, w_s, w_r, r1_r, r2_r, rxa_r, rx_r, rs_s, ag_s, ag_r,
 ):
     s = lax.axis_index("seq")
@@ -68,18 +68,19 @@
         (joined.at[:, pl.ds(512, 256)], kvbuf.at[s, 0]),
         (joined.at[:, pl.ds(0, 256)], qbuf.at[0]),
         (joined.at[:, pl.ds(256, 256)], qbuf.at[1]),
-        (gu, guv),
+        (gu.at[:, 0, :], guv.at[0]),
         (ow, owv),
         (hid.at[pl.ds(al(own_block * BLK, 16), BLK), :], hidv),
         (dw, dwv),
         (nw, nwv),
         (joined.at[:, pl.ds(768, 256)], kvbuf.at[s, 1]),
+        (gu.at[:, 1, :], guv.at[1]),
     ]
     local_copies = [
         pltpu.make_async_copy(src, dst, lsem.at[i]) for i, (src, dst) in enumerate(loads)
     ]
-    for copy in local_copies:
-        copy.start()
+    for i in (0, 8, 3, 9, 1, 2):
+        local_copies[i].start()
 
     def rcopy(src, dst, send, recv, dev):
         return pltpu.make_async_remote_copy(
@@ -103,7 +104,10 @@
     kv_sent = []
     for part in range(2):
         local_copies[(0, 8)[part]].wait()
-        for ok, dev in ((z < 3, zup), (x == 0, xnb), (z == 0, zdn), (c == 0, sib)):
+        outs = [(z < 3, zup), (x == 0, xnb), (z == 0, zdn), (c == 0, sib)]
+        if part == 1:
+            outs.append(((x == 0) & (z >= 2), zdn))
+        for ok, dev in outs:
             sem = len(kv_sent)
             kv_sent.append((ok, s, part, dev))
 
@@ -112,9 +116,12 @@
                 kv_send(s, part, dev, sem).start()
 
     local_copies[3].wait()
+    local_copies[9].wait()
+    for i in (4, 5, 6, 7):
+        local_copies[i].start()
     for k in range(8):
         for m in range(2):
-            gub[k, m] = guv[:, m, k * UNITS : (k + 1) * UNITS].astype(BF)
+            gub[k, m] = guv[m, :, k * UNITS : (k + 1) * UNITS].astype(BF)
 
     def a_send(k):
         peer = (t + k) % 8
@@ -125,44 +132,45 @@
 
     local_copies[1].wait()
     local_copies[2].wait()
-    mbuf[...] = jnp.full(mbuf.shape, NEG, F32)
-    lbuf[...] = jnp.zeros(lbuf.shape, F32)
-    acc[...] = jnp.zeros(acc.shape, F32)
-
     end0 = lens[0]
     end1 = end0 + lens[1]
     end2 = end1 + lens[2]
 
-    def flash(slot):
-        place = s * ROWS + lax.broadcasted_iota(jnp.int32, (ROWS, 1), 0)
-        low = jnp.where(
-            place >= end2,
-            end2,
-            jnp.where(place >= end1, end1, jnp.where(place >= end0, end0, 0)),
-        )
+    place = s * ROWS + lax.broadcasted_iota(jnp.int32, (ROWS, 1), 0)
+    low = jnp.where(
+        place >= end2,
+        end2,
+        jnp.where(place >= end1, end1, jnp.where(place >= end0, end0, 0)),
+    )
+    lowbuf[...] = low
+
+    def flash(slot, own):
         other = slot * ROWS + lax.broadcasted_iota(jnp.int32, (ROWS, ROWS), 1)
-        allowed = (other >= low) & (other <= place)
-
-        def head(r, carry):
+        allowed = other >= lowbuf[...]
+        if own:
+            allowed = allowed & (other <= place)
+        for r in range(2):
             scores = lax.dot_general(
                 qbuf[r],
                 kvbuf[slot, 0],
                 (((1,), (1,)), ((), ())),
                 preferred_element_type=F32,
-            ) * (HD ** -0.5)
+            ) * (HD ** -0.5 * 1.4426950408889634)
             scores = jnp.where(allowed, scores, NEG)
-            before = mbuf[r]
-            peak = jnp.maximum(before, jnp.max(scores, axis=-1, keepdims=True))
-            weights = jnp.exp(scores - peak)
-            fade = jnp.exp(before - peak)
-            lbuf[r] = lbuf[r] * fade + jnp.sum(weights, axis=-1, keepdims=True)
+            peak = jnp.max(scores, axis=-1, keepdims=True)
+            if not own:
+                before = mbuf[r]
+                peak = jnp.maximum(before, peak)
+            weights = jnp.exp2(scores - peak)
+            total = jnp.sum(weights, axis=-1, keepdims=True)
+            blend = jnp.dot(weights.astype(BF), kvbuf[slot, 1], preferred_element_type=F32)
+            if not own:
+                fade = jnp.exp2(before - peak)
+                total = total + lbuf[r] * fade
+                blend = blend + acc[r] * fade
+            lbuf[r] = total
             mbuf[r] = peak
-            acc[r] = acc[r] * fade + jnp.dot(
-                weights.astype(BF), kvbuf[slot, 1], preferred_element_type=F32
-            )
-            return carry
-
-        lax.fori_loop(0, 2, head, 0)
+            acc[r] = blend
 
     def up_ok(off):
         return z + off >= 0
@@ -203,19 +211,19 @@
     def w_first():
         for m in range(2):
             w_go(s, m, xnb)
+        w_go(s, 0, zup)
+        w_go(s, 1, zup)
         for m in range(2):
             w_go(s, m, sib)
 
     def w_second():
-        w_go(s, 0, zup)
         w_go(s, 1, zdn)
-        w_go(s, 1, zup)
         w_go(s, 0, zdn)
 
     def comm_of(entries):
         plan = []
         for part, (cond, slot, forward, relays) in entries:
-            sends = relays + [(cond if forward is None else cond & forward, sib)]
+            sends = relays + [(cond if forward is None else cond & forward, sib)] * (forward is not False)
             numbered = []
             for ok, dev in sends:
                 numbered.append((ok, dev, len(kv_sent)))
@@ -241,13 +249,16 @@
     up1 = (up_ok(-1), up_slot(-1, c), None, [(middle, zup)])
     over = (down_ok(0), down_slot(0, c), c == 1, [((x == 1) & (z >= 1), zdn), ((x == 1) & (z == 3), zup)])
     down1 = (down_ok(1), down_slot(1, c), None, [((x == 1) & middle, zdn)])
+    down1v = (down_ok(1), down_slot(1, c), None, [])
+    side1 = ((x == 0) & middle, down_slot(1, c), False, [((x == 0) & middle, zdn)])
+    side2 = ((x == 0) & (z <= 1), down_slot(2, c), False, [((x == 0) & (z <= 1), xnb)])
     up3 = (up_ok(-3), up_slot(-3, c), None, [])
     down3 = (down_ok(3), down_slot(3, c), None, [])
     up2 = (up_ok(-2), up_slot(-2, c), None, [])
     down2 = (down_ok(2), down_slot(2, c), None, [])
-    comm_a = comm_of([(0, over), (0, up1), (1, over), (1, up1)])
-    comm_b0 = comm_of([(0, down1)])
-    comm_b1 = comm_of([(1, down1), (0, up3), (1, up3), (0, down3), (1, down3)])
+    comm_a = comm_of([(0, over), (0, up1), (1, side1), (1, over), (1, up1)])
+    comm_b0 = comm_of([(0, down1), (1, side2)])
+    comm_b1 = comm_of([(1, down1v), (0, up3), (1, up3), (0, down3), (1, down3)])
     comm_c = comm_of([(0, up2), (0, down2), (1, up2), (1, down2)])
 
     offsets = {2: -1, 3: 0, 4: -1, 5: 0, 6: 1, 7: -3, 8: 3, 9: 1, 10: -3, 11: 3, 12: -2, 13: 2, 14: -2, 15: 2}
@@ -291,11 +302,12 @@
 
         @pl.when(ok)
         def _():
-            flash(slot)
+            flash(slot, False)
 
         return carry
 
-    lax.fori_loop(0, 16, step, 0)
+    flash(s, True)
+    lax.fori_loop(1, 16, step, 0)
 
     for r in range(2):
         att[:, r * HD : (r + 1) * HD] = (acc[r] / lbuf[r, :, 0:1]).astype(BF)
@@ -308,44 +320,50 @@
     s_xzp = (1 - x) * 8 + zp * 2 + c
     s_xz2 = (1 - x) * 8 + (z + 2) % 4 * 2 + c
 
+    def w_share(slot, *halves):
+        for m in halves:
+            w_arrived(slot, m)
+            w_go(slot, m, sib)
+
+    def w_early():
+        w_arrived(s_zm, 0)
+        w_go(s_zm, 0, zup)
+        w_go(s_zm, 0, sib)
+        w_arrived(s_zp, 1)
+        w_go(s_zp, 1, zdn)
+
     def w_over():
-        for m in range(2):
-            w_arrived(s_x, m)
+        w_arrived(s_x, 0)
         w_go(s_x, 0, zup)
+        w_arrived(s_x, 1)
         w_go(s_x, 1, zdn)
         w_go(s_x, 1, zup)
         w_go(s_x, 0, zdn)
-        for m in range(2):
-            w_go(s_x, m, sib)
-
-    def w_relay():
-        w_arrived(s_zm, 0)
-        w_go(s_zm, 0, zup)
-        w_arrived(s_zp, 1)
-        w_go(s_zp, 1, zdn)
-        w_arrived(s_zm, 1)
-        w_arrived(s_zp, 0)
-        for slot in (s_zm, s_zp):
-            for m in range(2):
-                w_go(slot, m, sib)
-
-    def w_relay_over():
+        w_go(s_x, 0, sib)
+        w_go(s_x, 1, sib)
+        w_go(s_zp, 1, sib)
+
+    def w_rest():
+        w_share(s_zm, 1)
+        w_share(s_zp, 0)
+        w_share(s_z2, 0)
+        w_arrived(s_z2, 1)
+        w_go(s_z2, 1, sib)
+
+    def w_late():
         w_arrived(s_xzm, 0)
         w_go(s_xzm, 0, zup)
+        w_go(s_xzm, 0, sib)
         w_arrived(s_xzp, 1)
         w_go(s_xzp, 1, zdn)
-        w_arrived(s_xzm, 1)
-        w_arrived(s_xzp, 0)
-        for m in range(2):
-            w_arrived(s_z2, m)
-        for slot in (s_xzm, s_xzp, s_z2):
-            for m in range(2):
-                w_go(slot, m, sib)
+        w_go(s_xzp, 1, sib)
+
+    def w_last():
+        w_share(s_xzp, 0)
+        w_share(s_xzm, 1)
 
     def w_end():
-        for m in range(2):
-            w_arrived(s_xz2, m)
-            w_go(s_xz2, m, sib)
+        w_share(s_xz2, 0, 1)
         for xx in range(2):
             for zz in range(4):
                 for m in range(2):
@@ -424,7 +442,7 @@
         at = rows_of(h * 4 + yy)
         pb[at, first] = (pb[at, first].astype(F32) + rxa[k, yy].astype(F32)).astype(BF)
 
-    def tp_sum(k, lhs, weight, pb, pump0, pump1):
+    def tp_sum(k, lhs, weight, pb, pump0, pump2, pump1):
         project(lhs, weight, o, pb)
         rs_over(k, pb)
         rs_far(k, pb, 0)
@@ -438,6 +456,7 @@
         rs_near(k, pb, 1)
         sx[k] = rs_end(k, pb, 0).astype(BF)
         send(sx.at[k], rx.at[k], rx_r.at[k], xhi)
+        pump2()
         rs_middle(k, pb, 1)
         rs_add(k, pb, yp)
         rs_add(k, pb, ym)
@@ -538,13 +557,12 @@
         pass
 
     local_copies[4].wait()
-    w_over()
-    total = tp_sum(0, att, owv, pb1, nothing, w_relay)
+    total = tp_sum(0, att, owv, pb1, w_early, w_over, w_rest)
     local_copies[5].wait()
     mid = hidv[...].astype(F32) + normed(total, g_attn)
     resid[...] = mid
     ag1[rows_of(own_block), :] = normed(mid, g_pre).astype(BF)
-    tp_gather(0, ag1, nothing, w_relay_over)
+    tp_gather(0, ag1, w_late, w_last)
     w_end()
 
     def ffn(g):
@@ -564,7 +582,7 @@
     tp_gathered(0, ag1)
     ffn(o)
     local_copies[6].wait()
-    total = tp_sum(1, act, dwv, pb2, nothing, nothing)
+    total = tp_sum(1, act, dwv, pb2, nothing, nothing, nothing)
     last = resid[...] + normed(total, g_post)
     ag2[rows_of(own_block), :] = normed(last, g_next).astype(BF)
     tp_gather(1, ag2, nothing, nothing)
@@ -611,10 +629,11 @@
         V(dw.shape, BF),
         V(nw.shape, BF),
         V((BLK, D), BF),
-        V((PIECE, 2, gu.shape[2]), F32),
+        V((2, PIECE, gu.shape[2]), F32),
         V((8, 2, PIECE, UNITS), BF),
         V((8, 2, PIECE, UNITS), BF),
         V((2, D, UNITS), BF),
+        V((ROWS, 1), jnp.int32),
         V((2, ROWS, 1), F32),
         V((2, ROWS, 1), F32),
         V((2, ROWS, HD), F32),
@@ -632,7 +651,7 @@
         V((ROWS, D), BF),
         V((ROWS, UNITS), BF),
         V((BLK, D), F32),
-        DMA((9,)),
+        DMA((10,)),
         DMA((36,)),
         DMA((16, 2)),
         DMA((8,)),

time: 150 us -> 147 us (0.980)
  Pallas kernels: 146 us -> 144 us
    pallas_call x1, Pallas kernels: 146 us -> 144 us  [local(): pl.pallas_call(kernel, out_shape=jax.ShapeDtypeStruct((ROWS, QKV), BF), i...]
where the time goes in v5:
time: 147 us; the launch traced here: 146 us
  Pallas kernels  144 us (98%)
  local copies, waits for them, and re-layouts  2.06 us (1%)
    pallas_call x1, Pallas kernels, local(): pl.pallas_call(kernel, out_shape=jax.ShapeDtypeStruct((ROWS, QKV), BF), i...  144 us

profile of v5, /device:TPU:1, one launch (start us, length us, event | category | flops | bytes accessed | tf_op | source)
XLA Modules:
  0.0 146.4 jit_solution(16420978828289460412)
XLA Ops:
  0.0 144.4 %shard_map.109 = bf16[384,1024]{1,0:T(8,128)(2,1)} custom-call(s32[4]{0:T(128)} %lens.1, bf16[384,3584]{1,0:T(8,128)(2,1)} %hid.1, bf16[384,1024]{1,0:T(8,128)(2,1)} %joined.1, bf16[512,3584]{1,0:T(8,128)(2,1)} %ow.1, f32[28,2,7168]{2,1,0:T(2,128)} %bitcast.1, bf16[896,3584]{1,0:T(8,128)(2,1)} %dw.1, bf16[3584,1024]{1,0:T(8,128)(2,1)} %nw.1, f32[3584]{0:T(1024)} %g_attn.1, ...), custom_call_target="tpu_custom_call" | custom-call | tf_op jit(solution)/shard_map/pallas_call | solution.py:669
  144.4 2.1 %copy.13 = bf16[384,1024]{1,0:T(8,128)(2,1)} copy(bf16[384,1024]{1,0:T(8,128)(2,1)} %shard_map.109) | data formatting | bytes 1572864

commit v6 on v5

--- a/solution.py
+++ b/solution.py
@@ -79,7 +79,7 @@
     local_copies = [
         pltpu.make_async_copy(src, dst, lsem.at[i]) for i, (src, dst) in enumerate(loads)
     ]
-    for i in (0, 8, 3, 9, 1, 2):
+    for i in (0, 8, 9, 3, 1, 2):
         local_copies[i].start()
 
     def rcopy(src, dst, send, recv, dev):
@@ -115,20 +115,18 @@
             def _(part=part, dev=dev, sem=sem):
                 kv_send(s, part, dev, sem).start()
 
-    local_copies[3].wait()
-    local_copies[9].wait()
+    def a_send(k, m):
+        peer = (t + k) % 8
+        return rcopy(gub.at[peer, m], abuf.at[t, m], a_s.at[k, m], a_r.at[k, m], (s, peer))
+
+    for m in (1, 0):
+        local_copies[(3, 9)[m]].wait()
+        for k in range(8):
+            gub[k, m] = guv[m, :, k * UNITS : (k + 1) * UNITS].astype(BF)
+        for k in range(1, 8):
+            a_send(k, m).start()
     for i in (4, 5, 6, 7):
         local_copies[i].start()
-    for k in range(8):
-        for m in range(2):
-            gub[k, m] = guv[m, :, k * UNITS : (k + 1) * UNITS].astype(BF)
-
-    def a_send(k):
-        peer = (t + k) % 8
-        return rcopy(gub.at[peer], abuf.at[t], a_s.at[k], a_r.at[k], (s, peer))
-
-    for k in range(1, 8):
-        a_send(k).start()
 
     local_copies[1].wait()
     local_copies[2].wait()
@@ -199,26 +197,25 @@
     def w_arrived(slot, m):
         w_copy(slot, m, sib, 0).wait_recv()
 
-    def repack():
+    def repack(m):
         for k in range(1, 8):
             peer = (t + 8 - k) % 8
-            rcopy(gub.at[0], abuf.at[peer], a_s.at[k], a_r.at[k], (s, peer)).wait_recv()
-        abuf[t] = gub[t]
-        for m in range(2):
-            rows = jnp.concatenate([abuf[k, m].astype(F32) for k in range(8)], axis=0)
-            wbuf[m, pl.ds(al(s * CHUNK, 16), CHUNK), :] = rows.astype(BF)
+            rcopy(gub.at[0, m], abuf.at[peer, m], a_s.at[k, m], a_r.at[k, m], (s, peer)).wait_recv()
+        abuf[t, m] = gub[t, m]
+        rows = jnp.concatenate([abuf[k, m].astype(F32) for k in range(8)], axis=0)
+        wbuf[m, pl.ds(al(s * CHUNK, 16), CHUNK), :] = rows.astype(BF)
 
     def w_first():
-        for m in range(2):
-            w_go(s, m, xnb)
+        repack(1)
+        w_go(s, 1, zdn)
+        w_go(s, 1, xnb)
+        repack(0)
         w_go(s, 0, zup)
+        w_go(s, 0, zdn)
+        w_go(s, 0, xnb)
         w_go(s, 1, zup)
         for m in range(2):
             w_go(s, m, sib)
-
-    def w_second():
-        w_go(s, 1, zdn)
-        w_go(s, 0, zdn)
 
     def comm_of(entries):
         plan = []
@@ -271,13 +268,11 @@
         @pl.when(i == 4)
         def _():
             comm_b0()
-            repack()
             w_first()
 
         @pl.when(i == 6)
         def _():
             comm_b1()
-            w_second()
 
         @pl.when(i == 12)
         def _():
@@ -333,10 +328,10 @@
         w_go(s_zp, 1, zdn)
 
     def w_over():
+        w_arrived(s_x, 1)
+        w_go(s_x, 1, zdn)
         w_arrived(s_x, 0)
         w_go(s_x, 0, zup)
-        w_arrived(s_x, 1)
-        w_go(s_x, 1, zdn)
         w_go(s_x, 1, zup)
         w_go(s_x, 0, zdn)
         w_go(s_x, 0, sib)
@@ -609,7 +604,8 @@
             kv_send(slot, part, dev, sem).wait_send()
 
     for k in range(1, 8):
-        a_send(k).wait_send()
+        for m in range(2):
+            a_send(k, m).wait_send()
     for sem, (slot, m, dev) in enumerate(w_sent):
         w_copy(slot, m, dev, sem).wait_send()
     for copy in rs_sent + ag_sent:
@@ -654,8 +650,8 @@
         DMA((10,)),
         DMA((36,)),
         DMA((16, 2)),
-        DMA((8,)),
-        DMA((8,)),
+        DMA((8, 2)),
+        DMA((8, 2)),
         DMA((48,)),
         DMA((16, 2)),
         DMA((2, 3, 2)),

time: 147 us -> 146 us (level)
  no operation moved by 1% of the time
where the time goes in v6:
time: 146 us
  Pallas kernels  144 us (99%)
  local copies, waits for them, and re-layouts  2.06 us (1%)
    pallas_call x1, Pallas kernels, local(): pl.pallas_call(kernel, out_shape=jax.ShapeDtypeStruct((ROWS, QKV), BF), i...  144 us

profile of v6, /device:TPU:1, one launch (start us, length us, event | category | flops | bytes accessed | tf_op | source)
XLA Modules:
  0.0 145.9 jit_solution(16917322716485622235)
XLA Ops:
  0.0 143.9 %shard_map.109 = bf16[384,1024]{1,0:T(8,128)(2,1)} custom-call(s32[4]{0:T(128)} %lens.1, bf16[384,3584]{1,0:T(8,128)(2,1)} %hid.1, bf16[384,1024]{1,0:T(8,128)(2,1)} %joined.1, bf16[512,3584]{1,0:T(8,128)(2,1)} %ow.1, f32[28,2,7168]{2,1,0:T(2,128)} %bitcast.1, bf16[896,3584]{1,0:T(8,128)(2,1)} %dw.1, bf16[3584,1024]{1,0:T(8,128)(2,1)} %nw.1, f32[3584]{0:T(1024)} %g_attn.1, ...), custom_call_target="tpu_custom_call" | custom-call | tf_op jit(solution)/shard_map/pallas_call | solution.py:665
  143.9 2.1 %copy.13 = bf16[384,1024]{1,0:T(8,128)(2,1)} copy(bf16[384,1024]{1,0:T(8,128)(2,1)} %shard_map.109) | data formatting | bytes 1572864
